TPU v7x, 32 devices: a whole 2x2x4 slice. The times are simulated.
32 devices in a mesh: dom: 8 (over z, y), lev: 4 (over x, core).
Axes of the slice: x: 2, y: 2, z: 4, core: 2. Of those that a mesh axis runs over, the one named last changes fastest.
Arguments:
- state: float32 [2, 32, 8192], P(None, 'lev', 'dom'), may hold values from -6 to 6
- neighbours: int32 [7, 8192], P(None, 'dom'), may hold values from -1 to 1279, as said below
- edge_coef: float32 [7, 8192], P(None, 'dom'), may hold values from 0.05 to 0.45
- send_lists: int32 [8, 2, 128], P('dom'), may hold values from 0 to 1023, as said below
- vert_coef: float32 [2], replicated, may hold values from 0.1 to 0.45
- w_lw: bfloat16 [64, 4096], replicated, may hold values from -0.75 to 0.75
- w_sw: bfloat16 [64, 4096], replicated, may hold values from -0.75 to 0.75
- g_weight: float32 [2, 128], replicated, may hold values from 0.25 to 4
- day: int32 [8192], P(('dom', 'lev')), may hold values from 0 to 1, as said below
- cos_zenith: float32 [8192], P(('dom', 'lev')), may hold values from 0.05 to 1
- owner_map: int32 [8192], P(('dom', 'lev')), may hold values from 0 to 511, as said below
Outputs:
- new_state: float32 [2, 32, 8192], P(None, 'lev', 'dom')
- heating: bfloat16 [32, 8192], P(None, ('dom', 'lev'))
- owner_flux: float32 [16384], P(('dom', 'lev'))
Inputs may be any that keep to these rules, and one draw needn't show every extreme that they name: `neighbours`: entries are -1 (padding, after 5 to 7 valid entries of a cell) or an index into the partition's extended numbering: own cells, then 128 cells from the west partition, then 128 from the east; every halo position is named by some cell. `send_lists`: each row holds 128 distinct local cell numbers of the sending partition. `day`: the daylit columns form one run of consecutive column numbers, wrapping around at the end, that holds half of all columns. `owner_map`: the 256 columns of one device (aligned blocks along the cells) take distinct slots; at most 64 columns of one device go to one owner, and one owner receives 64 from every device; each owner's share of a device's daylit columns is in proportion to the slots it receives from that device.
All inputs are finite; a program needn't handle non-finite values.
Results may differ from a plain program's by a relative error of at most 0.005.
Values may be sent and summed in bfloat16 or wider, within the bound.
No kernel may reach another device: no remote copies, remote signals or barrier semaphores. Data moves between devices by JAX's collectives and lax.ppermute only.
A program may use at most 64 MiB of HBM per device.

v0:
```python
import jax
import jax.numpy as jnp
from jax import lax
from jax.sharding import PartitionSpec as P

LEVELS = 32
G = 128
NEIGH = 7


def padded(block, sides, width, periodic):
    for axis, dim in sides:
        count = lax.axis_size(axis)
        forward = [(i, i + 1) for i in range(count - 1)]
        if periodic:
            forward.append((count - 1, 0))
        backward = [(target, source) for source, target in forward]
        low = lax.ppermute(
            lax.slice_in_dim(block, block.shape[dim] - width, None, axis=dim), axis, forward
        )
        high = lax.ppermute(lax.slice_in_dim(block, 0, width, axis=dim), axis, backward)
        block = jnp.concatenate([low, block, high], axis=dim)
    return block


def tendency(fields, neighbours, edge_coef, send_lists, vert_coef):
    halo_cells = send_lists.shape[2]
    outgoing = jnp.concatenate(
        [jnp.take(fields, send_lists[0, 0], axis=2), jnp.take(fields, send_lists[0, 1], axis=2)],
        axis=2,
    )
    bordered = padded(outgoing, (("dom", 2),), halo_cells, True)
    extended = jnp.concatenate(
        [fields, bordered[:, :, :halo_cells], bordered[:, :, 3 * halo_cells :]], axis=2
    )
    valid = neighbours >= 0
    weights = jnp.where(valid, edge_coef, 0.0)
    safe_links = jnp.where(valid, neighbours, 0)
    total = jnp.zeros_like(fields)
    for neighbour in range(NEIGH):
        picked = jnp.take(extended, safe_links[neighbour], axis=2)
        total = total + weights[neighbour] * (picked - fields)
    stacked = padded(fields, (("lev", 1),), 1, False)
    total = total + vert_coef[:, None, None] * (stacked[:, 2:] - 2.0 * fields + stacked[:, :-2])
    return total


def radiate(features, sun, w_lw, w_sw, g_weight):
    heats = []
    bottoms = []
    for band_index, weight in enumerate((w_lw, w_sw)):
        optical = lax.dot_general(
            weight, features, (((0,), (0,)), ((), ())), preferred_element_type=jnp.float32
        )
        optical = jax.nn.softplus(optical).reshape(LEVELS, G, -1) * (1.5 / LEVELS)
        summed = jnp.cumsum(optical, axis=0)
        absorbed = jnp.exp(optical - summed) - jnp.exp(-summed)
        heats.append(LEVELS / G * jnp.einsum("g,lgn->ln", g_weight[band_index], absorbed))
        bottoms.append(jnp.einsum("g,gn->n", g_weight[band_index], jnp.exp(-summed[-1])) / G)
    return (sun[None, :] * heats[1] - heats[0], bottoms[0] + sun * bottoms[1])


def radiate_blocks(features, sun, w_lw, w_sw, g_weight):
    total_cols = features.shape[1]
    block_cols = 256
    blocks = total_cols // block_cols
    feature_blocks = features.reshape(features.shape[0], blocks, block_cols).transpose(1, 0, 2)
    sun_blocks = sun.reshape(blocks, block_cols)

    def one_block(pair):
        return radiate(pair[0], pair[1], w_lw, w_sw, g_weight)

    heat_blocks, bottom_blocks = lax.map(one_block, (feature_blocks, sun_blocks))
    return (
        heat_blocks.transpose(1, 0, 2).reshape(LEVELS, total_cols),
        bottom_blocks.reshape(total_cols),
    )


def on_device(
    state,
    neighbours,
    edge_coef,
    send_lists,
    vert_coef,
    w_lw,
    w_sw,
    g_weight,
    day,
    cos_zenith,
    owner_map,
):
    middle = state + tendency(state, neighbours, edge_coef, send_lists, vert_coef) / 3.0
    new_state = state + tendency(middle, neighbours, edge_coef, send_lists, vert_coef) * 0.5
    columns = lax.all_to_all(
        new_state.astype(jnp.bfloat16), "lev", split_axis=2, concat_axis=1, tiled=True
    )
    column_count = columns.shape[2]
    slot_total = 2 * column_count
    sun = (day.astype(jnp.float32) * cos_zenith).astype(jnp.bfloat16)
    packed = jnp.zeros((2, LEVELS, slot_total), jnp.bfloat16).at[:, :, owner_map].set(columns)
    marks = jnp.zeros((2, 1, slot_total), jnp.bfloat16)
    marks = marks.at[0, 0, owner_map].set(jnp.ones((column_count,), jnp.bfloat16))
    marks = marks.at[1, 0, owner_map].set(sun)
    arrived, arrived_marks = (
        lax.all_to_all(packed, "dom", split_axis=2, concat_axis=2, tiled=True),
        lax.all_to_all(marks, "dom", split_axis=2, concat_axis=2, tiled=True),
    )
    heat_owner, bottom = radiate_blocks(
        arrived.reshape(2 * LEVELS, slot_total),
        arrived_marks[1, 0].astype(jnp.float32),
        w_lw,
        w_sw,
        g_weight,
    )
    owner_flux = bottom * arrived_marks[0, 0].astype(jnp.float32)
    returned = lax.all_to_all(
        heat_owner.astype(jnp.bfloat16), "dom", split_axis=1, concat_axis=1, tiled=True
    )
    heating = jnp.take(returned, owner_map, axis=1)
    return (new_state, heating, owner_flux)


def solution(mesh):
    placed = (
        P(None, "lev", "dom"),
        P(None, "dom"),
        P(None, "dom"),
        P("dom", None, None),
        P(),
        P(),
        P(),
        P(),
        P(("dom", "lev")),
        P(("dom", "lev")),
        P(("dom", "lev")),
    )
    return jax.shard_map(
        on_device,
        mesh=mesh,
        in_specs=placed,
        out_specs=(P(None, "lev", "dom"), P(None, ("dom", "lev")), P(("dom", "lev"))),
        check_vma=False,
    )
```

profile of v0, /device:TPU:0, one launch (start us, length us, event | category | flops | bytes accessed | tf_op | source)
XLA Modules:
  0.0 306.9 jit_solution(1357336886428639390)
XLA Ops:
  55.9 4.7 %collective-permute-start.5 = (f32[2,8,128]{2,1,0:T(8,128)S(1)}, f32[2,8,128]{2,1,0:T(8,128)S(1)}, u32[]{:S(2)}, u32[]{:S(2)}) collective-permute-start(f32[2,8,128]{2,1,0:T(8,128)S(1)} %select_bitcast_fusion.3), channel_id=1, source_target_pairs={{4,0},{8,4},{12,8},{16,12},{20,16},{24,20},{28,24},{0,28},{5,1},{9... | collective-permute-start | bytes 24584 | tf_op jit(solution)/shard_map/ppermute | solution.py:21
  73.5 7.6 %gather_fusion.16 = f32[1024,2,8]{2,1,0:T(2,128)} fusion(f32[2,8,1280]{1,0,2:T(2,128)S(1)} %copy.454, s32[1024]{0:T(1024)} %copy-done.13), kind=kCustom, calls=%fused_computation.15.clone | custom fusion | bytes 135168 | tf_op jit(solution)/shard_map/jit(_take)/gather | solution.py:41
  81.1 7.6 %gather_fusion.15 = f32[1024,2,8]{2,1,0:T(2,128)} fusion(f32[2,8,1280]{1,0,2:T(2,128)S(1)} %copy.454, s32[1024]{0:T(1024)} %copy-done.16), kind=kCustom, calls=%fused_computation.14.clone | custom fusion | bytes 135168 | tf_op jit(solution)/shard_map/jit(_take)/gather | solution.py:41
  88.7 7.6 %gather_fusion.14 = f32[1024,2,8]{2,1,0:T(2,128)} fusion(f32[2,8,1280]{1,0,2:T(2,128)S(1)} %copy.454, s32[1024]{0:T(1024)} %copy-done.14), kind=kCustom, calls=%fused_computation.13.clone | custom fusion | bytes 135168 | tf_op jit(solution)/shard_map/jit(_take)/gather | solution.py:41
  96.4 7.6 %gather_fusion.13 = f32[1024,2,8]{2,1,0:T(2,128)} fusion(f32[2,8,1280]{1,0,2:T(2,128)S(1)} %copy.454, s32[1024]{0:T(1024)} %copy-done.11), kind=kCustom, calls=%fused_computation.12.clone | custom fusion | bytes 135168 | tf_op jit(solution)/shard_map/jit(_take)/gather | solution.py:41
  104.0 7.7 %gather_fusion.12 = f32[1024,2,8]{2,1,0:T(2,128)} fusion(f32[2,8,1280]{1,0,2:T(2,128)S(1)} %copy.454, s32[1024]{0:T(1024)} %copy-done.12), kind=kCustom, calls=%fused_computation.11.clone | custom fusion | bytes 135168 | tf_op jit(solution)/shard_map/jit(_take)/gather | solution.py:41
  122.0 5.2 %all-to-all-start = ((bf16[4,2,2048]{2,1,0:T(2,128)(2,1)}), bf16[4,2,2048]{2,1,0:T(2,128)(2,1)S(1)}, u32[]{:S(2)}, u32[]{:S(2)}) async-start(bf16[4,2,2048]{2,1,0:T(2,128)(2,1)} %reshape.304), calls=%async_computation | async-start | bytes 65536 | tf_op jit(solution)/shard_map/all_to_all | solution.py:95
  127.9 12.4 %scatter_fusion.1 = bf16[2,512]{1,0:T(2,128)(2,1)S(1)} fusion(bf16[2,512]{1,0:T(2,128)(2,1)S(1)} %broadcast.79, s32[256]{0:T(256)S(1)} %bitcast.315, bf16[256]{0:T(256)(128)(2,1)S(1)} %broadcast.101), kind=kCustom, calls=%fused_computation.20 | custom fusion | bytes 3584 | tf_op jit(solution)/shard_map/scatter | solution.py:103
  140.3 12.4 %scatter_fusion.2 = bf16[2,512]{1,0:T(2,128)(2,1)S(1)} fusion(bf16[2,512]{1,0:T(2,128)(2,1)S(1)} %scatter_fusion.1, s32[256]{0:T(256)S(1)} %bitcast.314, bf16[256]{0:T(256)(128)(2,1)S(1)} %multiply_convert_fusion), kind=kCustom, calls=%fused_computation.21 | custom fusion | bytes 3584 | tf_op jit(solution)/shard_map/scatter | solution.py:104
  158.4 7.3 %scatter_fusion = bf16[2,32,512]{1,0,2:T(2,128)(2,1)S(1)} fusion(bf16[2,32,512]{1,0,2:T(2,128)(2,1)S(1)} %broadcast_in_dim.75, s32[256]{0:T(256)S(1)} %copy-done.18, bf16[256,2,32]{2,1,0:T(2,128)(2,1)S(1)} %copy.475), kind=kCustom, calls=%fused_computation.19 | custom fusion | bytes 99328 | tf_op jit(solution)/shard_map/scatter | solution.py:101
  166.9 5.6 %all-to-all-start.1 = ((bf16[8,2,2048]{2,1,0:T(2,128)(2,1)}), bf16[8,2,2048]{2,1,0:T(2,128)(2,1)S(1)}, u32[]{:S(2)}, u32[]{:S(2)}) async-start(bf16[8,2,2048]{2,1,0:T(2,128)(2,1)} %reshape.306), calls=%async_computation.1 | async-start | bytes 131072 | tf_op jit(solution)/shard_map/all_to_all | solution.py:106
  179.8 114.3 %while.12 = (s32[]{:T(128)}, bf16[2,32,256]{2,1,0:T(8,128)(2,1)S(1)}, f32[2,256]{1,0:T(2,128)S(1)}, bf16[2,64,256]{2,1,0:T(8,128)(2,1)S(1)}, bf16[64,4096]{1,0:T...) while((s32[]{:T(128)}, ...), condition=%wide.region_6.9_spmd, body=%wide.region_3.8_spmd.sunk | while | flops 360932608 | bytes 127514808 | solution.py:73
  179.9 4.6 %fusion.124 = f32[4096,256]{0,1:T(8,128)} fusion(bf16[64,4096]{1,0:T(8,128)(2,1)S(1)} %get-tuple-element.275, bf16[2,64,256]{2,1,0:T(8,128)(2,1)S(1)} %get-tuple-element.271, s32[]{:T(128)S(6)} %copy.523), kind=kOutput, calls=%fused_computation.27.clone.1 | convolution fusion | flops 141557760 | bytes 4751364 | tf_op jit(solution)/shard_map/while/body/eval_jaxpr/dot_general | solution.py:52
  184.5 4.7 %fusion.127 = f32[4096,256]{0,1:T(8,128)} fusion(bf16[64,4096]{1,0:T(8,128)(2,1)S(1)} %get-tuple-element.272, bf16[2,64,256]{2,1,0:T(8,128)(2,1)S(1)} %get-tuple-element.271, s32[]{:T(128)S(6)} %copy.523), kind=kOutput, calls=%fused_computation.26.clone.1 | convolution fusion | flops 141557760 | bytes 4751364 | tf_op jit(solution)/shard_map/while/body/eval_jaxpr/dot_general | solution.py:52
  189.1 5.7 %copy.511 = f32[4096,256]{1,0:T(8,128)} copy(f32[4096,256]{0,1:T(8,128)} %fusion.127) | data formatting | bytes 8388608 | tf_op jit(solution)/shard_map/while/body/eval_jaxpr/mul | solution.py:55
  199.3 5.7 %copy.512 = f32[4096,256]{0,1:T(8,128)} copy(f32[4096,256]{1,0:T(8,128)} %bitcast.309) | data formatting | bytes 8388608 | tf_op jit(solution)/shard_map/while/body/eval_jaxpr/jit(cumsum)/reduce_window_sum | solution.py:56
  213.0 5.7 %copy.507 = f32[4096,256]{1,0:T(8,128)} copy(f32[4096,256]{0,1:T(8,128)} %fusion.124) | data formatting | bytes 8388608 | tf_op jit(solution)/shard_map/while/body/eval_jaxpr/mul | solution.py:55
  223.4 5.7 %copy.508 = f32[4096,256]{0,1:T(8,128)} copy(f32[4096,256]{1,0:T(8,128)} %bitcast.308) | data formatting | bytes 8388608 | tf_op jit(solution)/shard_map/while/body/eval_jaxpr/jit(cumsum)/reduce_window_sum | solution.py:56
  241.6 4.7 %fusion.127 = f32[4096,256]{0,1:T(8,128)} fusion(bf16[64,4096]{1,0:T(8,128)(2,1)S(1)} %get-tuple-element.272, bf16[2,64,256]{2,1,0:T(8,128)(2,1)S(1)} %get-tuple-element.271, s32[]{:T(128)S(6)} %copy.523), kind=kOutput, calls=%fused_computation.26.clone.1 | convolution fusion | flops 141557760 | bytes 4751364 | tf_op jit(solution)/shard_map/while/body/eval_jaxpr/dot_general | solution.py:52
  246.3 5.7 %copy.511 = f32[4096,256]{1,0:T(8,128)} copy(f32[4096,256]{0,1:T(8,128)} %fusion.127) | data formatting | bytes 8388608 | tf_op jit(solution)/shard_map/while/body/eval_jaxpr/mul | solution.py:55
  256.5 5.7 %copy.512 = f32[4096,256]{0,1:T(8,128)} copy(f32[4096,256]{1,0:T(8,128)} %bitcast.309) | data formatting | bytes 8388608 | tf_op jit(solution)/shard_map/while/body/eval_jaxpr/jit(cumsum)/reduce_window_sum | solution.py:56
  270.1 5.7 %copy.507 = f32[4096,256]{1,0:T(8,128)} copy(f32[4096,256]{0,1:T(8,128)} %fusion.124) | data formatting | bytes 8388608 | tf_op jit(solution)/shard_map/while/body/eval_jaxpr/mul | solution.py:55
  280.5 5.7 %copy.508 = f32[4096,256]{0,1:T(8,128)} copy(f32[4096,256]{1,0:T(8,128)} %bitcast.308) | data formatting | bytes 8388608 | tf_op jit(solution)/shard_map/while/body/eval_jaxpr/jit(cumsum)/reduce_window_sum | solution.py:56
  299.0 6.0 %all-to-all-done.3 = bf16[8,2,1024]{2,1,0:T(2,128)(2,1)S(1)} async-done(((bf16[8,2,1024]{2,1,0:T(2,128)(2,1)}), bf16[8,2,1024]{2,1,0:T(2,128)(2,1)S(1)}, u32[]{:S(2)}, u32[]{:S(2)}) %all-to-all-start.3) | async-done | bytes 32800 | tf_op jit(solution)/shard_map/all_to_all | solution.py:117
  (223 shorter events, 153.9 us)
Async XLA Ops:
  1.6 51.8 %collective-permute-start.3 = (f32[2,1,1024]{2,0,1:T(2,128)S(1)}, f32[2,1,1024]{2,0,1:T(2,128)S(1)}, u32[]{:S(2)}, u32[]{:S(2)}) collective-permute-start(f32[2,1,1024]{2,0,1:T(2,128)S(1)} %copy.491), channel_id=1, source_target_pairs={{0,1},{1,2},{2,3},{4,5},{5,6},{6,7},{8,9},{9,10},{10,11},{12,13},{... | collective-permute-start | bytes 24584 | tf_op jit(solution)/shard_map/ppermute | solution.py:18
  4.0 49.5 %collective-permute-start.2 = (f32[2,1,1024]{2,0,1:T(2,128)S(1)}, f32[2,1,1024]{2,0,1:T(2,128)S(1)}, u32[]{:S(2)}, u32[]{:S(2)}) collective-permute-start(f32[2,1,1024]{2,0,1:T(2,128)S(1)} %copy.490), channel_id=1, source_target_pairs={{1,0},{2,1},{3,2},{5,4},{6,5},{7,6},{9,8},{10,9},{11,10},{13,12},{... | collective-permute-start | bytes 24584 | tf_op jit(solution)/shard_map/ppermute | solution.py:21
  8.2 9.1 %collective-permute-start = (f32[2,8,128]{1,0,2:T(2,128)S(1)}, f32[2,8,128]{1,0,2:T(2,128)S(1)}, u32[]{:S(2)}, u32[]{:S(2)}) collective-permute-start(f32[2,8,128]{1,0,2:T(2,128)S(1)} %select_bitcast_fusion.1), channel_id=1, source_target_pairs={{0,4},{4,8},{8,12},{12,16},{16,20},{20,24},{24,28},{28,0},{1,5},{5... | collective-permute-start | bytes 24584 | tf_op jit(solution)/shard_map/ppermute | solution.py:18
  11.6 9.1 %collective-permute-start.1 = (f32[2,8,128]{1,0,2:T(2,128)S(1)}, f32[2,8,128]{1,0,2:T(2,128)S(1)}, u32[]{:S(2)}, u32[]{:S(2)}) collective-permute-start(f32[2,8,128]{1,0,2:T(2,128)S(1)} %select_bitcast_fusion), channel_id=1, source_target_pairs={{4,0},{8,4},{12,8},{16,12},{20,16},{24,20},{28,24},{0,28},{5,1},{9... | collective-permute-start | bytes 24584 | tf_op jit(solution)/shard_map/ppermute | solution.py:21
  15.5 37.9 %copy-start.19 = (pred[1024]{0:T(1024)(128)(4,1)}, pred[1024]{0:T(1024)(128)(4,1)S(1)}, u32[]{:S(2)}) copy-start(pred[1024]{0:T(1024)(128)(4,1)S(1)} %compare_and_fusion.6) | copy-start | bytes 3076
  15.6 37.9 %copy-start.20 = (pred[1024]{0:T(1024)(128)(4,1)}, pred[1024]{0:T(1024)(128)(4,1)S(1)}, u32[]{:S(2)}) copy-start(pred[1024]{0:T(1024)(128)(4,1)S(1)} %get-tuple-element.189) | copy-start | bytes 3076
  15.6 37.9 %copy-start.21 = (pred[1024]{0:T(1024)(128)(4,1)}, pred[1024]{0:T(1024)(128)(4,1)S(1)}, u32[]{:S(2)}) copy-start(pred[1024]{0:T(1024)(128)(4,1)S(1)} %get-tuple-element.190) | copy-start | bytes 3076
  15.7 37.8 %copy-start.22 = (pred[1024]{0:T(1024)(128)(4,1)}, pred[1024]{0:T(1024)(128)(4,1)S(1)}, u32[]{:S(2)}) copy-start(pred[1024]{0:T(1024)(128)(4,1)S(1)} %get-tuple-element.191) | copy-start | bytes 3076
  15.7 37.8 %copy-start.23 = (pred[1024]{0:T(1024)(128)(4,1)}, pred[1024]{0:T(1024)(128)(4,1)S(1)}, u32[]{:S(2)}) copy-start(pred[1024]{0:T(1024)(128)(4,1)S(1)} %get-tuple-element.192) | copy-start | bytes 3076
  15.8 37.7 %copy-start.24 = (pred[1024]{0:T(1024)(128)(4,1)}, pred[1024]{0:T(1024)(128)(4,1)S(1)}, u32[]{:S(2)}) copy-start(pred[1024]{0:T(1024)(128)(4,1)S(1)} %get-tuple-element.193) | copy-start | bytes 3076
  15.8 37.7 %copy-start.25 = (pred[1024]{0:T(1024)(128)(4,1)}, pred[1024]{0:T(1024)(128)(4,1)S(1)}, u32[]{:S(2)}) copy-start(pred[1024]{0:T(1024)(128)(4,1)S(1)} %get-tuple-element.194) | copy-start | bytes 3076
  55.9 9.3 %collective-permute-start.4 = (f32[2,8,128]{2,1,0:T(8,128)S(1)}, f32[2,8,128]{2,1,0:T(8,128)S(1)}, u32[]{:S(2)}, u32[]{:S(2)}) collective-permute-start(f32[2,8,128]{2,1,0:T(8,128)S(1)} %select_bitcast_fusion.4), channel_id=1, source_target_pairs={{0,4},{4,8},{8,12},{12,16},{16,20},{20,24},{24,28},{28,0},{1,5},{5... | collective-permute-start | bytes 24584 | tf_op jit(solution)/shard_map/ppermute | solution.py:18
  55.9 9.2 %collective-permute-start.5 = (f32[2,8,128]{2,1,0:T(8,128)S(1)}, f32[2,8,128]{2,1,0:T(8,128)S(1)}, u32[]{:S(2)}, u32[]{:S(2)}) collective-permute-start(f32[2,8,128]{2,1,0:T(8,128)S(1)} %select_bitcast_fusion.3), channel_id=1, source_target_pairs={{4,0},{8,4},{12,8},{16,12},{20,16},{24,20},{28,24},{0,28},{5,1},{9... | collective-permute-start | bytes 24584 | tf_op jit(solution)/shard_map/ppermute | solution.py:21
  61.9 55.5 %collective-permute-start.7 = (f32[2,1,1024]{2,0,1:T(2,128)}, f32[2,1,1024]{2,0,1:T(2,128)}, u32[]{:S(2)}, u32[]{:S(2)}) collective-permute-start(f32[2,1,1024]{2,0,1:T(2,128)} %copy.470), channel_id=1, source_target_pairs={{0,1},{1,2},{2,3},{4,5},{5,6},{6,7},{8,9},{9,10},{10,11},{12,13},{... | collective-permute-start | bytes 24584 | tf_op jit(solution)/shard_map/ppermute | solution.py:18
  63.9 54.2 %collective-permute-start.6 = (f32[2,1,1024]{2,0,1:T(2,128)}, f32[2,1,1024]{2,0,1:T(2,128)}, u32[]{:S(2)}, u32[]{:S(2)}) collective-permute-start(f32[2,1,1024]{2,0,1:T(2,128)} %copy.468), channel_id=1, source_target_pairs={{1,0},{2,1},{3,2},{5,4},{6,5},{7,6},{9,8},{10,9},{11,10},{13,12},{... | collective-permute-start | bytes 24584 | tf_op jit(solution)/shard_map/ppermute | solution.py:21
  116.5 40.6 %copy-start.27 = (s32[256]{0:T(256)S(1)}, s32[256]{0:T(256)}, u32[]{:S(2)}) copy-start(s32[256]{0:T(256)} %param.27) | copy-start | bytes 3076
  116.5 40.6 %copy-start.30 = (f32[2,128]{1,0:T(2,128)S(1)}, f32[2,128]{1,0:T(2,128)}, u32[]{:S(2)}) copy-start(f32[2,128]{1,0:T(2,128)} %param.24) | copy-start | bytes 3076
  116.9 41.5 %copy-start.18 = (s32[256]{0:T(256)S(1)}, s32[256]{0:T(256)}, u32[]{:S(2)}) copy-start(s32[256]{0:T(256)} %copy-done.17) | copy-start | bytes 3076
  118.8 61.0 %copy-start.28 = (bf16[64,4096]{1,0:T(8,128)(2,1)S(1)}, bf16[64,4096]{1,0:T(8,128)(2,1)}, u32[]{:S(2)}) copy-start(bf16[64,4096]{1,0:T(8,128)(2,1)} %param.23) | copy-start | bytes 1572868
  118.8 61.0 %copy-start.29 = (bf16[64,4096]{1,0:T(8,128)(2,1)S(1)}, bf16[64,4096]{1,0:T(8,128)(2,1)}, u32[]{:S(2)}) copy-start(bf16[64,4096]{1,0:T(8,128)(2,1)} %param.22) | copy-start | bytes 1572868
  122.0 31.6 %all-to-all-start = ((bf16[4,2,2048]{2,1,0:T(2,128)(2,1)}), bf16[4,2,2048]{2,1,0:T(2,128)(2,1)S(1)}, u32[]{:S(2)}, u32[]{:S(2)}) async-start(bf16[4,2,2048]{2,1,0:T(2,128)(2,1)} %reshape.304), calls=%async_computation | async-start | bytes 65536 | tf_op jit(solution)/shard_map/all_to_all | solution.py:95
  153.6 13.2 %all-to-all-start.2 = ((bf16[2,1,512]{0,1,2:T(2,128)(2,1)}), bf16[2,1,512]{0,1,2:T(2,128)(2,1)S(1)}, u32[]{:S(2)}, u32[]{:S(2)}) async-start(bf16[2,1,512]{0,1,2:T(2,128)(2,1)} %copy.477), calls=%async_computation.2 | async-start | bytes 524288 | tf_op jit(solution)/shard_map/all_to_all | solution.py:107
  166.9 12.5 %all-to-all-start.1 = ((bf16[8,2,2048]{2,1,0:T(2,128)(2,1)}), bf16[8,2,2048]{2,1,0:T(2,128)(2,1)S(1)}, u32[]{:S(2)}, u32[]{:S(2)}) async-start(bf16[8,2,2048]{2,1,0:T(2,128)(2,1)} %reshape.306), calls=%async_computation.1 | async-start | bytes 131072 | tf_op jit(solution)/shard_map/all_to_all | solution.py:106
  295.1 10.0 %all-to-all-start.3 = ((bf16[8,2,1024]{2,1,0:T(2,128)(2,1)}), bf16[8,2,1024]{2,1,0:T(2,128)(2,1)S(1)}, u32[]{:S(2)}, u32[]{:S(2)}) async-start(bf16[8,2,1024]{2,1,0:T(2,128)(2,1)} %reshape.308), calls=%async_computation.3 | async-start | bytes 65536 | tf_op jit(solution)/shard_map/all_to_all | solution.py:117
  (21 other events, 461.6 us)
where the time goes:
time: 309 us; the launch traced here: 307 us
  local copies, waits for them, and re-layouts  184 us (60%)
  other arithmetic  42.7 us (14%)
  starting transfers between devices  34.8 us (11%)
  matrix products  30.3 us (10%)
  waiting for transfers between devices  13.5 us (4%)
    gather x28, local copies, waits for them, and re-layouts, tendency(): picked = jnp.take(extended, safe_links[neighbour], axis=2)  79.3 us
    mul x4, local copies, waits for them, and re-layouts, radiate(): optical = jax.nn.softplus(optical).reshape(LEVELS, G, -1) * (1.5 / LEVELS)  22.8 us
    another operation x4, local copies, waits for them, and re-layouts, radiate(): summed = jnp.cumsum(optical, axis=0)  22.7 us
    dot_general x4, matrix products, radiate(): lax.dot_general(weight, features, (((0,), (0,)), ((), ())), preferred_ele...  18.6 us
    while x4, other arithmetic  18.3 us
    scatter x2, local copies, waits for them, and re-layouts, on_device(): marks = marks.at[1, 0, owner_map].set(sun)  13.3 us
    scatter x1, local copies, waits for them, and re-layouts, on_device(): marks.at[0, 0, owner_map].set(jnp.ones((column_count,), jnp.bfloat16))  12.4 us
    dot_general x4, matrix products, radiate(): jnp.einsum('g,lgn->ln', g_weight[band_index], absorbed)  11.2 us
  transfers between devices with their start and end apart: 12, of which 4 were waited for; matrix products, arithmetic and copies ran while one was open for 43% of the time, Pallas kernels for 0%

commit v1 on v0

v1 whole, which is shorter than its diff:
```python
import functools
import math

import jax
import jax.numpy as jnp
from jax import lax
from jax.experimental import pallas as pl
from jax.experimental.pallas import tpu as pltpu
from jax.sharding import PartitionSpec as P

NEIGH = 7
LOG2E = 1.0 / math.log(2.0)


def padded(block, sides, width, periodic):
    for axis, dim in sides:
        count = lax.axis_size(axis)
        forward = [(i, i + 1) for i in range(count - 1)]
        if periodic:
            forward.append((count - 1, 0))
        backward = [(target, source) for source, target in forward]
        low = lax.ppermute(
            lax.slice_in_dim(block, block.shape[dim] - width, None, axis=dim), axis, forward
        )
        high = lax.ppermute(lax.slice_in_dim(block, 0, width, axis=dim), axis, backward)
        block = jnp.concatenate([low, block, high], axis=dim)
    return block


def tendency(fields, neighbours, edge_coef, send_lists, vert_coef):
    halo_cells = send_lists.shape[2]
    outgoing = jnp.concatenate(
        [jnp.take(fields, send_lists[0, 0], axis=2), jnp.take(fields, send_lists[0, 1], axis=2)],
        axis=2,
    )
    bordered = padded(outgoing, (("dom", 2),), halo_cells, True)
    extended = jnp.concatenate(
        [fields, bordered[:, :, :halo_cells], bordered[:, :, 3 * halo_cells :]], axis=2
    )
    valid = neighbours >= 0
    weights = jnp.where(valid, edge_coef, 0.0)
    safe_links = jnp.where(valid, neighbours, 0)
    total = jnp.zeros_like(fields)
    for neighbour in range(NEIGH):
        picked = jnp.take(extended, safe_links[neighbour], axis=2)
        total = total + weights[neighbour] * (picked - fields)
    stacked = padded(fields, (("lev", 1),), 1, False)
    total = total + vert_coef[:, None, None] * (stacked[:, 2:] - 2.0 * fields + stacked[:, :-2])
    return total


def radiate_kernel(
    levels, feat_ref, sun_ref, owner_ref, wlw_ref, wsw_ref, gw_ref, heat_ref, flux_ref, acc, gwb, tot
):
    cols = feat_ref.shape[1]
    spectral = gw_ref.shape[1]
    owners, cap = flux_ref.shape
    groups = spectral // 8
    chunk = 16
    scale = -1.5 / levels * LOG2E
    for b in range(2):
        wide = jnp.broadcast_to(gw_ref[b : b + 1, :], (spectral, spectral))
        gwb[b] = jnp.transpose(wide)
        tot[b, 0] = jnp.broadcast_to(
            jnp.sum(gwb[b].reshape(groups, 8, spectral), axis=0)[:, :1], (8, cols)
        )
        acc[b] = jnp.zeros((spectral, cols), jnp.float32)

    def level(l, carry):
        for b, w_ref in enumerate((wlw_ref, wsw_ref)):
            w = w_ref[:, pl.ds(pl.multiple_of(l * spectral, spectral), spectral)]
            x = lax.dot_general(
                w, feat_ref[...], (((0,), (0,)), ((), ())), preferred_element_type=jnp.float32
            )
            part = jnp.zeros((8, cols), jnp.float32)
            for r in range(0, spectral, chunk):
                xs = x[r : r + chunk]
                e = jnp.exp2(jnp.abs(xs) * -LOG2E)
                total = acc[b, r : r + chunk] + (jnp.maximum(xs, 0.0) + jnp.log(1.0 + e))
                acc[b, r : r + chunk] = total
                passed = jnp.exp2(total * scale)
                weight = jnp.concatenate([gwb[b, r : r + chunk]] * (cols // spectral), axis=1)
                passed = passed * weight
                for i in range(0, chunk, 8):
                    part = part + passed[i : i + 8]
            tot[b, l + 1] = part
        return carry

    lax.fori_loop(0, levels, level, 0)
    sun = sun_ref[...]
    fraction = levels / spectral
    heats = []
    for b in range(2):
        heats.append(fraction * jnp.sum(tot[b, :levels] - tot[b, 1:], axis=1))
    heat_ref[...] = (sun * heats[1] - heats[0]).astype(jnp.bfloat16)
    bottoms = [jnp.sum(tot[b, levels], axis=0, keepdims=True) / spectral for b in range(2)]
    surface = bottoms[0] + sun * bottoms[1]
    scatter(surface, owner_ref[...], flux_ref, owners, cap, cols)


def scatter(surface, slot, flux_ref, owners, cap, cols):
    high = surface.astype(jnp.bfloat16).astype(jnp.float32)
    rest = surface - high
    mid = rest.astype(jnp.bfloat16).astype(jnp.float32)
    low = rest - mid
    owner = slot // cap
    within = slot - owner * cap
    mine = lax.broadcasted_iota(jnp.int32, (owners, cols), 0) == owner
    terms = jnp.concatenate([jnp.where(mine, term, 0.0) for term in (high, mid, low)], axis=0)
    place = lax.broadcasted_iota(jnp.int32, (cap, cols), 0) == within
    place = jnp.where(place, 1.0, 0.0).astype(jnp.bfloat16)
    out = lax.dot_general(
        terms.astype(jnp.bfloat16),
        place,
        (((1,), (1,)), ((), ())),
        preferred_element_type=jnp.float32,
    )
    flux_ref[...] = (out[:owners] + out[owners : 2 * owners]) + out[2 * owners :]


def radiate(features, sun, owner_map, w_lw, w_sw, g_weight, owners):
    cols = features.shape[1]
    spectral = g_weight.shape[1]
    levels = w_lw.shape[1] // spectral
    cap = 2 * cols // owners
    vmem = pl.BlockSpec(memory_space=pltpu.VMEM)
    return pl.pallas_call(
        functools.partial(radiate_kernel, levels),
        in_specs=[vmem] * 6,
        out_specs=[vmem] * 2,
        out_shape=[
            jax.ShapeDtypeStruct((levels, cols), jnp.bfloat16),
            jax.ShapeDtypeStruct((owners, cap), jnp.float32),
        ],
        scratch_shapes=[
            pltpu.VMEM((2, spectral, cols), jnp.float32),
            pltpu.VMEM((2, spectral, spectral), jnp.float32),
            pltpu.VMEM((2, levels + 1, 8, cols), jnp.float32),
        ],
        name="radiate",
    )(features, sun, owner_map, w_lw, w_sw, g_weight)


def on_device(
    state,
    neighbours,
    edge_coef,
    send_lists,
    vert_coef,
    w_lw,
    w_sw,
    g_weight,
    day,
    cos_zenith,
    owner_map,
):
    middle = state + tendency(state, neighbours, edge_coef, send_lists, vert_coef) / 3.0
    new_state = state + tendency(middle, neighbours, edge_coef, send_lists, vert_coef) * 0.5
    columns = lax.all_to_all(
        new_state.astype(jnp.bfloat16), "lev", split_axis=2, concat_axis=1, tiled=True
    )
    cols = columns.shape[2]
    sun = (day.astype(jnp.float32) * cos_zenith).astype(jnp.bfloat16).astype(jnp.float32)
    heating, flux = radiate(
        columns.reshape(-1, cols),
        sun.reshape(1, cols),
        owner_map.reshape(1, cols),
        w_lw,
        w_sw,
        g_weight,
        lax.axis_size("dom"),
    )
    owner_flux = lax.all_to_all(flux, "dom", split_axis=0, concat_axis=0, tiled=True)
    return (new_state, heating, owner_flux.reshape(-1))


def solution(mesh):
    placed = (
        P(None, "lev", "dom"),
        P(None, "dom"),
        P(None, "dom"),
        P("dom", None, None),
        P(),
        P(),
        P(),
        P(),
        P(("dom", "lev")),
        P(("dom", "lev")),
        P(("dom", "lev")),
    )
    return jax.shard_map(
        on_device,
        mesh=mesh,
        in_specs=placed,
        out_specs=(P(None, "lev", "dom"), P(None, ("dom", "lev")), P(("dom", "lev"))),
        check_vma=False,
    )
```

time: 309 us -> 150 us (0.49)
  local copies, waits for them, and re-layouts: 184 us -> 90.7 us
  other arithmetic: 42.7 us -> 8.07 us
  matrix products: 30.3 us -> 0 us
  Pallas kernels: 0 us -> 12.3 us
  starting transfers between devices: 34.8 us -> 23.6 us
  waiting for transfers between devices: 13.5 us -> 3.34 us
  blocking collectives: 0 us -> 9.65 us
    scatter x4 -> x0, local copies, waits for them, and re-layouts: 33 us -> none  [the longest x2 13.3 us: on_device(): marks = marks.at[1, 0, owner_map].set(sun)]
    dot_general x12 -> x0, matrix products: 30.3 us -> none  [the longest x4 18.6 us: radiate(): lax.dot_general(weight, features, (((0,), (0,)), ((), ())), preferred_ele...]
    mul x4 -> x0, local copies, waits for them, and re-layouts: 22.8 us -> none  [radiate(): optical = jax.nn.softplus(optical).reshape(LEVELS, G, -1) * (1.5 / LEVELS)]
    another operation x5 -> x0, local copies, waits for them, and re-layouts: 22.7 us -> none  [the longest x4 22.7 us: radiate(): summed = jnp.cumsum(optical, axis=0)]
    while x4 -> x0, other arithmetic: 18.3 us -> none
    all_to_all x3 -> x0, starting transfers between devices: 12.4 us -> none  [the longest x1 5.63 us: on_device(): lax.all_to_all(packed, 'dom', split_axis=2, concat_axis=2, tiled=True)]
    pallas_call x0 -> x1, Pallas kernels: none -> 12.3 us  [radiate(): pl.pallas_call(functools.partial(radiate_kernel, levels), in_specs=[vmem]...]
    all_to_all x3 -> x0, waiting for transfers between devices: 10.2 us -> none  [the longest x1 6.02 us: on_device(): lax.all_to_all(heat_owner.astype(jnp.bfloat16), 'dom', split_axis=1, conc...]
  transfers between devices with their start and end apart: 12 -> 9, of which waited for: 4 -> 1; matrix products, arithmetic and copies ran while one was open for 43% -> 58% of each run, Pallas kernels for 0% -> 0%
where the time goes in v1:
time: 150 us; the launch traced here: 149 us
  local copies, waits for them, and re-layouts  90.7 us (60%)
  starting transfers between devices  23.6 us (16%)
  Pallas kernels  12.3 us (8%)
  blocking collectives  9.65 us (6%)
  other arithmetic  8.07 us (5%)
  waiting for transfers between devices  3.34 us (2%)
  between operations  1.59 us (1%)
    gather x28, local copies, waits for them, and re-layouts, tendency(): picked = jnp.take(extended, safe_links[neighbour], axis=2)  77.2 us
    pallas_call x1, Pallas kernels, radiate(): pl.pallas_call(functools.partial(radiate_kernel, levels), in_specs=[vmem]...  12.3 us
    ppermute x4, starting transfers between devices, padded(): lax.ppermute(lax.slice_in_dim(block, 0, width, axis=dim), axis, backward)  10.4 us
    ppermute x4, starting transfers between devices, padded(): lax.ppermute(lax.slice_in_dim(block, block.shape[dim] - width, None, axis...  9.89 us
    all_to_all x1, blocking collectives, on_device(): lax.all_to_all(flux, 'dom', split_axis=0, concat_axis=0, tiled=True)  9.65 us
    concatenate x2, other arithmetic, tendency(): jnp.concatenate([fields, bordered[:, :, :halo_cells], bordered[:, :, 3 *...  4.65 us
    unnamed x83, local copies, waits for them, and re-layouts  4.03 us
    all_to_all x1, waiting for transfers between devices, on_device(): lax.all_to_all(new_state.astype(jnp.bfloat16), 'lev', split_axis=2, conca...  3.32 us
  transfers between devices with their start and end apart: 9, of which 1 were waited for; matrix products, arithmetic and copies ran while one was open for 58% of the time, Pallas kernels for 0%

profile of v1, /device:TPU:0, one launch (start us, length us, event | category | flops | bytes accessed | tf_op | source)
XLA Modules:
  0.0 149.2 jit_solution(1206946652487467266)
XLA Ops:
  3.7 3.0 %collective-permute-start = (f32[2,8,128]{1,0,2:T(2,128)S(1)}, f32[2,8,128]{1,0,2:T(2,128)S(1)}, u32[]{:S(2)}, u32[]{:S(2)}) collective-permute-start(f32[2,8,128]{1,0,2:T(2,128)S(1)} %select_bitcast_fusion.1), channel_id=1, source_target_pairs={{0,4},{4,8},{8,12},{12,16},{16,20},{20,24},{24,28},{28,0},{1,5},{5... | collective-permute-start | bytes 24584 | tf_op jit(solution)/shard_map/ppermute | solution.py:22
  7.6 3.1 %collective-permute-start.1 = (f32[2,8,128]{1,0,2:T(2,128)S(1)}, f32[2,8,128]{1,0,2:T(2,128)S(1)}, u32[]{:S(2)}, u32[]{:S(2)}) collective-permute-start(f32[2,8,128]{1,0,2:T(2,128)S(1)} %select_bitcast_fusion), channel_id=1, source_target_pairs={{4,0},{8,4},{12,8},{16,12},{20,16},{24,20},{28,24},{0,28},{5,1},{9... | collective-permute-start | bytes 24584 | tf_op jit(solution)/shard_map/ppermute | solution.py:25
  12.1 3.0 %collective-permute-start.3 = (f32[2,1,1024]{2,0,1:T(2,128)S(1)}, f32[2,1,1024]{2,0,1:T(2,128)S(1)}, u32[]{:S(2)}, u32[]{:S(2)}) collective-permute-start(f32[2,1,1024]{2,0,1:T(2,128)S(1)} %copy.281), channel_id=1, source_target_pairs={{0,1},{1,2},{2,3},{4,5},{5,6},{6,7},{8,9},{9,10},{10,11},{12,13},{... | collective-permute-start | bytes 24584 | tf_op jit(solution)/shard_map/ppermute | solution.py:22
  15.6 4.6 %pad_maximum_fusion = f32[2,8,1280]{1,0,2:T(2,128)S(1)} fusion(f32[2,8,128]{1,0,2:T(2,128)S(1)} %collective-permute-done.1, f32[2,8,128]{1,0,2:T(2,128)S(1)} %collective-permute-done, f32[2,8,1024]{1,0,2:T(2,128)S(1)} %copy.243), kind=kLoop, calls=%fused_computation.18 | loop fusion | flops 40960 | bytes 163840 | tf_op jit(solution)/shard_map/concatenate | solution.py:37
  20.3 3.5 %gather_fusion.2 = f32[1024,2,8]{2,1,0:T(2,128)S(1)} fusion(f32[2,8,1280]{1,0,2:T(2,128)S(1)} %pad_maximum_fusion, s32[1024]{0:T(1024)S(1)} %fusion.44), kind=kCustom, calls=%fused_computation.1.clone | custom fusion | bytes 135168 | tf_op jit(solution)/shard_map/jit(_take)/gather | solution.py:45
  24.2 3.6 %gather_fusion.3 = f32[1024,2,8]{2,1,0:T(2,128)S(1)} fusion(f32[2,8,1280]{1,0,2:T(2,128)S(1)} %pad_maximum_fusion, s32[1024]{0:T(1024)S(1)} %fusion.38), kind=kCustom, calls=%fused_computation.5.clone | custom fusion | bytes 135168 | tf_op jit(solution)/shard_map/jit(_take)/gather | solution.py:45
  28.2 3.6 %gather_fusion.4 = f32[1024,2,8]{2,1,0:T(2,128)S(1)} fusion(f32[2,8,1280]{1,0,2:T(2,128)S(1)} %pad_maximum_fusion, s32[1024]{0:T(1024)S(1)} %fusion.39), kind=kCustom, calls=%fused_computation.6.clone | custom fusion | bytes 135168 | tf_op jit(solution)/shard_map/jit(_take)/gather | solution.py:45
  32.2 3.6 %gather_fusion.5 = f32[1024,2,8]{2,1,0:T(2,128)S(1)} fusion(f32[2,8,1280]{1,0,2:T(2,128)S(1)} %pad_maximum_fusion, s32[1024]{0:T(1024)S(1)} %fusion.40), kind=kCustom, calls=%fused_computation.7.clone | custom fusion | bytes 135168 | tf_op jit(solution)/shard_map/jit(_take)/gather | solution.py:45
  36.2 3.6 %gather_fusion.6 = f32[1024,2,8]{2,1,0:T(2,128)S(1)} fusion(f32[2,8,1280]{1,0,2:T(2,128)S(1)} %pad_maximum_fusion, s32[1024]{0:T(1024)S(1)} %fusion.41), kind=kCustom, calls=%fused_computation.8.clone | custom fusion | bytes 135168 | tf_op jit(solution)/shard_map/jit(_take)/gather | solution.py:45
  40.2 3.5 %gather_fusion.7 = f32[1024,2,8]{2,1,0:T(2,128)S(1)} fusion(f32[2,8,1280]{1,0,2:T(2,128)S(1)} %pad_maximum_fusion, s32[1024]{0:T(1024)S(1)} %fusion.42), kind=kCustom, calls=%fused_computation.9.clone | custom fusion | bytes 135168 | tf_op jit(solution)/shard_map/jit(_take)/gather | solution.py:45
  44.2 3.5 %gather_fusion.8 = f32[1024,2,8]{2,1,0:T(2,128)S(1)} fusion(f32[2,8,1280]{1,0,2:T(2,128)S(1)} %pad_maximum_fusion, s32[1024]{0:T(1024)S(1)} %fusion.43), kind=kCustom, calls=%fused_computation.10.clone | custom fusion | bytes 135168 | tf_op jit(solution)/shard_map/jit(_take)/gather | solution.py:45
  50.7 4.7 %collective-permute-start.5 = (f32[2,8,128]{2,1,0:T(8,128)S(1)}, f32[2,8,128]{2,1,0:T(8,128)S(1)}, u32[]{:S(2)}, u32[]{:S(2)}) collective-permute-start(f32[2,8,128]{2,1,0:T(8,128)S(1)} %select_bitcast_fusion.2), channel_id=1, source_target_pairs={{4,0},{8,4},{12,8},{16,12},{20,16},{24,20},{28,24},{0,28},{5,1},{9... | collective-permute-start | bytes 24584 | tf_op jit(solution)/shard_map/ppermute | solution.py:25
  58.0 3.8 %collective-permute-start.7 = (f32[2,1,1024]{2,0,1:T(2,128)}, f32[2,1,1024]{2,0,1:T(2,128)}, u32[]{:S(2)}, u32[]{:S(2)}) collective-permute-start(f32[2,1,1024]{2,0,1:T(2,128)} %copy.275), channel_id=1, source_target_pairs={{0,1},{1,2},{2,3},{4,5},{5,6},{6,7},{8,9},{9,10},{10,11},{12,13},{... | collective-permute-start | bytes 24584 | tf_op jit(solution)/shard_map/ppermute | solution.py:22
  62.4 3.5 %gather_fusion.11 = f32[1024,2,8]{2,1,0:T(2,128)S(1)} fusion(f32[2,8,1280]{1,0,2:T(2,128)S(1)} %copy.259, s32[1024]{0:T(1024)S(1)} %fusion.44), kind=kCustom, calls=%fused_computation.11.clone | custom fusion | bytes 135168 | tf_op jit(solution)/shard_map/jit(_take)/gather | solution.py:45
  66.0 4.0 %gather_fusion.12 = f32[1024,2,8]{2,1,0:T(2,128)S(1)} fusion(f32[2,8,1280]{1,0,2:T(2,128)S(1)} %copy.259, s32[1024]{0:T(1024)} %copy-done.19), kind=kCustom, calls=%fused_computation.12.clone | custom fusion | bytes 135168 | tf_op jit(solution)/shard_map/jit(_take)/gather | solution.py:45
  70.0 7.7 %gather_fusion.13 = f32[1024,2,8]{2,1,0:T(2,128)} fusion(f32[2,8,1280]{1,0,2:T(2,128)S(1)} %copy.259, s32[1024]{0:T(1024)} %copy-done.18), kind=kCustom, calls=%fused_computation.13.clone | custom fusion | bytes 135168 | tf_op jit(solution)/shard_map/jit(_take)/gather | solution.py:45
  77.7 7.6 %gather_fusion.14 = f32[1024,2,8]{2,1,0:T(2,128)} fusion(f32[2,8,1280]{1,0,2:T(2,128)S(1)} %copy.259, s32[1024]{0:T(1024)} %copy-done.17), kind=kCustom, calls=%fused_computation.14.clone | custom fusion | bytes 135168 | tf_op jit(solution)/shard_map/jit(_take)/gather | solution.py:45
  85.3 7.6 %gather_fusion.15 = f32[1024,2,8]{2,1,0:T(2,128)} fusion(f32[2,8,1280]{1,0,2:T(2,128)S(1)} %copy.259, s32[1024]{0:T(1024)} %copy-done.16), kind=kCustom, calls=%fused_computation.15.clone | custom fusion | bytes 135168 | tf_op jit(solution)/shard_map/jit(_take)/gather | solution.py:45
  93.0 7.6 %gather_fusion.16 = f32[1024,2,8]{2,1,0:T(2,128)} fusion(f32[2,8,1280]{1,0,2:T(2,128)S(1)} %copy.259, s32[1024]{0:T(1024)} %copy-done.15), kind=kCustom, calls=%fused_computation.16.clone | custom fusion | bytes 135168 | tf_op jit(solution)/shard_map/jit(_take)/gather | solution.py:45
  100.6 7.7 %gather_fusion.17 = f32[1024,2,8]{2,1,0:T(2,128)} fusion(f32[2,8,1280]{1,0,2:T(2,128)S(1)} %copy.259, s32[1024]{0:T(1024)} %copy-done.14), kind=kCustom, calls=%fused_computation.17.clone | custom fusion | bytes 135168 | tf_op jit(solution)/shard_map/jit(_take)/gather | solution.py:45
  116.7 3.3 %all-to-all-start = ((bf16[4,2,2048]{2,1,0:T(2,128)(2,1)}), bf16[4,2,2048]{2,1,0:T(2,128)(2,1)S(1)}, u32[]{:S(2)}, u32[]{:S(2)}) async-start(bf16[4,2,2048]{2,1,0:T(2,128)(2,1)} %reshape.257), calls=%async_computation | async-start | bytes 65536 | tf_op jit(solution)/shard_map/all_to_all | solution.py:159
  120.5 3.3 %all-to-all-done = bf16[4,2,2048]{2,1,0:T(2,128)(2,1)S(1)} async-done(((bf16[4,2,2048]{2,1,0:T(2,128)(2,1)}), bf16[4,2,2048]{2,1,0:T(2,128)(2,1)S(1)}, u32[]{:S(2)}, u32[]{:S(2)}) %all-to-all-start) | async-done | bytes 32800 | tf_op jit(solution)/shard_map/all_to_all | solution.py:159
  125.4 12.3 %radiate.1 = (bf16[32,256]{1,0:T(8,128)(2,1)}, f32[8,64]{1,0:T(8,128)}) custom-call(bf16[64,256]{1,0:T(8,128)(2,1)} %bitcast.156, f32[1,256]{1,0:T(1,128)} %bitcast.185, s32[1,256]{1,0:T(1,128)} %bitcast.187, bf16[64,4096]{1,0:T(8,128)(2,1)} %wlw_ref.1, bf16[64,4096]{1,0:T(8,128)(2,1)} %wsw_ref.1, f32[2,128]{1,0:T(2,128)} %gw_ref.1), custom_call_target="tpu_custom_call" | custom-call | tf_op jit(solution)/shard_map/radiate/pallas_call | solution.py:127
  137.7 9.7 %all_to_all.24 = f32[8,1,64]{2,1,0:T(1,128)S(1)} all-to-all(f32[8,1,64]{2,1,0:T(1,128)} %bitcast.186), channel_id=1, replica_groups=mesh['dom'=8,'lev'=4] {'dom'}, dimensions={0} | all-to-all | bytes 4096 | tf_op jit(solution)/shard_map/all_to_all | solution.py:173
  (155 shorter events, 26.0 us)
Async XLA Ops:
  0.7 14.8 %copy-start.20 = (f32[7,1024]{1,0:T(8,128)S(1)}, f32[7,1024]{1,0:T(8,128)}, u32[]{:S(2)}) copy-start(f32[7,1024]{1,0:T(8,128)} %param.17) | copy-start | bytes 86020
  3.7 11.9 %collective-permute-start = (f32[2,8,128]{1,0,2:T(2,128)S(1)}, f32[2,8,128]{1,0,2:T(2,128)S(1)}, u32[]{:S(2)}, u32[]{:S(2)}) collective-permute-start(f32[2,8,128]{1,0,2:T(2,128)S(1)} %select_bitcast_fusion.1), channel_id=1, source_target_pairs={{0,4},{4,8},{8,12},{12,16},{16,20},{20,24},{24,28},{28,0},{1,5},{5... | collective-permute-start | bytes 24584 | tf_op jit(solution)/shard_map/ppermute | solution.py:22
  7.6 7.9 %collective-permute-start.1 = (f32[2,8,128]{1,0,2:T(2,128)S(1)}, f32[2,8,128]{1,0,2:T(2,128)S(1)}, u32[]{:S(2)}, u32[]{:S(2)}) collective-permute-start(f32[2,8,128]{1,0,2:T(2,128)S(1)} %select_bitcast_fusion), channel_id=1, source_target_pairs={{4,0},{8,4},{12,8},{16,12},{20,16},{24,20},{28,24},{0,28},{5,1},{9... | collective-permute-start | bytes 24584 | tf_op jit(solution)/shard_map/ppermute | solution.py:25
  10.8 37.4 %collective-permute-start.2 = (f32[2,1,1024]{2,0,1:T(2,128)S(1)}, f32[2,1,1024]{2,0,1:T(2,128)S(1)}, u32[]{:S(2)}, u32[]{:S(2)}) collective-permute-start(f32[2,1,1024]{2,0,1:T(2,128)S(1)} %copy.280), channel_id=1, source_target_pairs={{1,0},{2,1},{3,2},{5,4},{6,5},{7,6},{9,8},{10,9},{11,10},{13,12},{... | collective-permute-start | bytes 24584 | tf_op jit(solution)/shard_map/ppermute | solution.py:25
  12.1 36.1 %collective-permute-start.3 = (f32[2,1,1024]{2,0,1:T(2,128)S(1)}, f32[2,1,1024]{2,0,1:T(2,128)S(1)}, u32[]{:S(2)}, u32[]{:S(2)}) collective-permute-start(f32[2,1,1024]{2,0,1:T(2,128)S(1)} %copy.281), channel_id=1, source_target_pairs={{0,1},{1,2},{2,3},{4,5},{5,6},{6,7},{8,9},{9,10},{10,11},{12,13},{... | collective-permute-start | bytes 24584 | tf_op jit(solution)/shard_map/ppermute | solution.py:22
  15.2 29.0 %copy-start.14 = (s32[1024]{0:T(1024)}, s32[1024]{0:T(1024)S(1)}, u32[]{:S(2)}) copy-start(s32[1024]{0:T(1024)S(1)} %fusion.43) | copy-start | bytes 12292
  15.3 33.0 %copy-start.21 = (pred[1024]{0:T(1024)(128)(4,1)}, pred[1024]{0:T(1024)(128)(4,1)S(1)}, u32[]{:S(2)}) copy-start(pred[1024]{0:T(1024)(128)(4,1)S(1)} %get-tuple-element.44) | copy-start | bytes 3076
  15.3 33.0 %copy-start.23 = (pred[1024]{0:T(1024)(128)(4,1)}, pred[1024]{0:T(1024)(128)(4,1)S(1)}, u32[]{:S(2)}) copy-start(pred[1024]{0:T(1024)(128)(4,1)S(1)} %get-tuple-element.45) | copy-start | bytes 3076
  15.3 24.5 %copy-start.16 = (s32[1024]{0:T(1024)}, s32[1024]{0:T(1024)S(1)}, u32[]{:S(2)}) copy-start(s32[1024]{0:T(1024)S(1)} %fusion.41) | copy-start | bytes 12292
  15.3 24.9 %copy-start.15 = (s32[1024]{0:T(1024)}, s32[1024]{0:T(1024)S(1)}, u32[]{:S(2)}) copy-start(s32[1024]{0:T(1024)S(1)} %fusion.42) | copy-start | bytes 12292
  15.3 32.9 %copy-start.25 = (pred[1024]{0:T(1024)(128)(4,1)}, pred[1024]{0:T(1024)(128)(4,1)S(1)}, u32[]{:S(2)}) copy-start(pred[1024]{0:T(1024)(128)(4,1)S(1)} %get-tuple-element.46) | copy-start | bytes 3076
  15.3 32.9 %copy-start.27 = (pred[1024]{0:T(1024)(128)(4,1)}, pred[1024]{0:T(1024)(128)(4,1)S(1)}, u32[]{:S(2)}) copy-start(pred[1024]{0:T(1024)(128)(4,1)S(1)} %get-tuple-element.47) | copy-start | bytes 3076
  15.4 24.4 %copy-start.17 = (s32[1024]{0:T(1024)}, s32[1024]{0:T(1024)S(1)}, u32[]{:S(2)}) copy-start(s32[1024]{0:T(1024)S(1)} %fusion.40) | copy-start | bytes 12292
  15.4 32.9 %copy-start.29 = (pred[1024]{0:T(1024)(128)(4,1)}, pred[1024]{0:T(1024)(128)(4,1)S(1)}, u32[]{:S(2)}) copy-start(pred[1024]{0:T(1024)(128)(4,1)S(1)} %get-tuple-element.48) | copy-start | bytes 3076
  15.4 32.9 %copy-start.31 = (pred[1024]{0:T(1024)(128)(4,1)}, pred[1024]{0:T(1024)(128)(4,1)S(1)}, u32[]{:S(2)}) copy-start(pred[1024]{0:T(1024)(128)(4,1)S(1)} %get-tuple-element.49) | copy-start | bytes 3076
  15.5 32.8 %copy-start.8 = (f32[1,1024]{1,0:T(1,128)}, f32[1,1024]{1,0:T(1,128)S(1)}, u32[]{:S(2)}) copy-start(f32[1,1024]{1,0:T(1,128)S(1)} %get-tuple-element.32) | copy-start | bytes 12292
  15.5 32.8 %copy-start.10 = (f32[1,1024]{1,0:T(1,128)}, f32[1,1024]{1,0:T(1,128)S(1)}, u32[]{:S(2)}) copy-start(f32[1,1024]{1,0:T(1,128)S(1)} %get-tuple-element.33) | copy-start | bytes 12292
  15.5 32.8 %copy-start.12 = (f32[1,1024]{1,0:T(1,128)}, f32[1,1024]{1,0:T(1,128)S(1)}, u32[]{:S(2)}) copy-start(f32[1,1024]{1,0:T(1,128)S(1)} %get-tuple-element.34) | copy-start | bytes 12292
  15.6 32.8 %copy-start.33 = (pred[1024]{0:T(1024)(128)(4,1)}, pred[1024]{0:T(1024)(128)(4,1)S(1)}, u32[]{:S(2)}) copy-start(pred[1024]{0:T(1024)(128)(4,1)S(1)} %compare_and_fusion.6) | copy-start | bytes 3076
  50.6 11.2 %collective-permute-start.4 = (f32[2,8,128]{2,1,0:T(8,128)S(1)}, f32[2,8,128]{2,1,0:T(8,128)S(1)}, u32[]{:S(2)}, u32[]{:S(2)}) collective-permute-start(f32[2,8,128]{2,1,0:T(8,128)S(1)} %select_bitcast_fusion.3), channel_id=1, source_target_pairs={{0,4},{4,8},{8,12},{12,16},{16,20},{20,24},{24,28},{28,0},{1,5},{5... | collective-permute-start | bytes 24584 | tf_op jit(solution)/shard_map/ppermute | solution.py:22
  50.7 11.1 %collective-permute-start.5 = (f32[2,8,128]{2,1,0:T(8,128)S(1)}, f32[2,8,128]{2,1,0:T(8,128)S(1)}, u32[]{:S(2)}, u32[]{:S(2)}) collective-permute-start(f32[2,8,128]{2,1,0:T(8,128)S(1)} %select_bitcast_fusion.2), channel_id=1, source_target_pairs={{4,0},{8,4},{12,8},{16,12},{20,16},{24,20},{28,24},{0,28},{5,1},{9... | collective-permute-start | bytes 24584 | tf_op jit(solution)/shard_map/ppermute | solution.py:25
  56.1 56.8 %collective-permute-start.6 = (f32[2,1,1024]{2,0,1:T(2,128)}, f32[2,1,1024]{2,0,1:T(2,128)}, u32[]{:S(2)}, u32[]{:S(2)}) collective-permute-start(f32[2,1,1024]{2,0,1:T(2,128)} %copy.273), channel_id=1, source_target_pairs={{1,0},{2,1},{3,2},{5,4},{6,5},{7,6},{9,8},{10,9},{11,10},{13,12},{... | collective-permute-start | bytes 24584 | tf_op jit(solution)/shard_map/ppermute | solution.py:25
  58.0 55.6 %collective-permute-start.7 = (f32[2,1,1024]{2,0,1:T(2,128)}, f32[2,1,1024]{2,0,1:T(2,128)}, u32[]{:S(2)}, u32[]{:S(2)}) collective-permute-start(f32[2,1,1024]{2,0,1:T(2,128)} %copy.275), channel_id=1, source_target_pairs={{0,1},{1,2},{2,3},{4,5},{5,6},{6,7},{8,9},{9,10},{10,11},{12,13},{... | collective-permute-start | bytes 24584 | tf_op jit(solution)/shard_map/ppermute | solution.py:22
  116.7 7.2 %all-to-all-start = ((bf16[4,2,2048]{2,1,0:T(2,128)(2,1)}), bf16[4,2,2048]{2,1,0:T(2,128)(2,1)S(1)}, u32[]{:S(2)}, u32[]{:S(2)}) async-start(bf16[4,2,2048]{2,1,0:T(2,128)(2,1)} %reshape.257), calls=%async_computation | async-start | bytes 65536 | tf_op jit(solution)/shard_map/all_to_all | solution.py:159
  (24 other events, 106.0 us)

commit v2 on v1

v2 whole, which is shorter than its diff:
```python
import functools
import math

import jax
import jax.numpy as jnp
from jax import lax
from jax.experimental import pallas as pl
from jax.experimental.pallas import tpu as pltpu
from jax.sharding import PartitionSpec as P

NEIGH = 7
LOG2E = 1.0 / math.log(2.0)


LANES = 128


def pick(tables, ids):
    within = ids & (LANES - 1)
    block = ids >> 7
    out = None
    for number, rows in tables.items():
        here = block == number
        found = [jnp.take_along_axis(r, within, axis=1, mode="promise_in_bounds") for r in rows]
        if out is None:
            out = [jnp.where(here, f, jnp.zeros_like(f)) for f in found]
        else:
            out = [jnp.where(here, f, o) for f, o in zip(found, out)]
    return out


def spread(row):
    return jnp.broadcast_to(row, (8, LANES))


def blocks_of(ref, count):
    return {
        t: [ref[v, :, t * LANES : (t + 1) * LANES] for v in range(2)] for t in range(count)
    }


def send_kernel(state_ref, nb_ref, coef_ref, lists_ref, near_a, near_b, far_a, far_b, own_ref, nb8, coef8):
    blocks = state_ref.shape[2] // LANES
    nb8[0:NEIGH] = nb_ref[...]
    nb8[NEIGH:8] = jnp.full((1, nb8.shape[1]), -1, jnp.int32)
    coef8[0:NEIGH] = coef_ref[...]
    coef8[NEIGH:8] = jnp.zeros((1, nb8.shape[1]), jnp.float32)
    tables = blocks_of(state_ref, blocks)
    packs = []
    for side in range(2):
        cells = spread(lists_ref[0, side : side + 1, :])
        out = pick(tables, cells)
        span = [slice(t * LANES, (t + 1) * LANES) for t in range(blocks)]
        near = pick({t: [nb8[:, span[t]]] for t in range(blocks)}, cells)[0]
        coef = pick({t: [coef8[:, span[t]]] for t in range(blocks)}, cells)[0]
        coef = jnp.where(near >= 0, coef, 0.0)
        total = jnp.sum(coef, axis=0, keepdims=True)
        part = [-total * o for o in out]
        for k in range(NEIGH):
            found = pick(tables, spread(near[k : k + 1]))
            part = [p + coef[k : k + 1] * f for p, f in zip(part, found)]
        packs.append((out, part, near.astype(jnp.float32), coef))
        for v in range(2):
            own_ref[side, v] = out[v]
    me = lax.axis_index("dom")
    even = me % 2 == 0
    early = me % 4 < 2
    west, east = packs
    for v in range(2):
        near_a[8 * v : 8 * v + 8] = jnp.where(even, east[0][v], west[0][v])
        near_b[8 * v : 8 * v + 8] = jnp.where(even, west[0][v], east[0][v])
        near_a[16 + 8 * v : 24 + 8 * v] = jnp.where(even, east[1][v], west[1][v])
        near_b[16 + 8 * v : 24 + 8 * v] = jnp.where(even, west[1][v], east[1][v])
        far_a[8 * v : 8 * v + 8] = jnp.where(early, east[0][v], west[0][v])
        far_b[8 * v : 8 * v + 8] = jnp.where(early, west[0][v], east[0][v])
    for i in range(2):
        near_a[32 + 8 * i : 40 + 8 * i] = jnp.where(even, east[2 + i], west[2 + i])
        near_b[32 + 8 * i : 40 + 8 * i] = jnp.where(even, west[2 + i], east[2 + i])


def spread_out(tables, nb_ref, coef_ref, at, start):
    for k in range(NEIGH):
        ids = nb_ref[k : k + 1, at]
        coef = jnp.where(ids >= 0, coef_ref[k : k + 1, at], 0.0)
        found = pick(tables, spread(ids))
        start = [s + coef * f for s, f in zip(start, found)]
    return start


def coef_total(nb_ref, coef_ref, at):
    return jnp.sum(jnp.where(nb_ref[:, at] >= 0, coef_ref[:, at], 0.0), axis=0, keepdims=True)


def inner_kernel(state_ref, nb_ref, coef_ref, y_ref):
    blocks = state_ref.shape[2] // LANES
    tables = blocks_of(state_ref, blocks)
    for t in range(blocks):
        at = slice(t * LANES, (t + 1) * LANES)
        total = coef_total(nb_ref, coef_ref, at)
        found = spread_out(tables, nb_ref, coef_ref, at, [-total * r for r in tables[t]])
        for v in range(2):
            y_ref[v, :, at] = found[v]


def vertical(f):
    rows = f.shape[0]
    zero = jnp.zeros_like(f[:1])
    up = jnp.concatenate([f[1:], zero], axis=0)
    down = jnp.concatenate([zero, f[: rows - 1]], axis=0)
    return up - 2.0 * f + down


def step_kernel(
    vert_ref, state_ref, nb_ref, coef_ref, y_ref, own_ref, near_a, near_b, far_a, far_b,
    part_ref, edge_ref, to1, to2, to3, t_own,
):
    cells = state_ref.shape[2]
    blocks = cells // LANES
    me = lax.axis_index("dom")
    even = me % 2 == 0
    early = me % 4 < 2
    west = jnp.where(even, near_b[...], near_a[...])
    east = jnp.where(even, near_a[...], near_b[...])
    far_west = jnp.where(early, far_b[...], far_a[...])
    far_east = jnp.where(early, far_a[...], far_b[...])
    halves = lambda a, start: [a[start : start + 8], a[start + 8 : start + 16]]
    own = [[own_ref[side, v] for v in range(2)] for side in range(2)]

    def rim(pack, tables):
        total = halves(pack, 16)
        ids = pack[32:40].astype(jnp.int32)
        for k in range(NEIGH):
            found = pick(tables, spread(ids[k : k + 1]))
            total = [s + pack[40 + k : 41 + k] * f for s, f in zip(total, found)]
        return [0.5 * s + y * (1.0 / 6.0) for s, y in zip(halves(pack, 0), total)]

    t_tables = {
        blocks: rim(west, {blocks: halves(far_west, 0), blocks + 1: own[0]}),
        blocks + 1: rim(east, {blocks: own[1], blocks + 1: halves(far_east, 0)}),
    }
    rim_tables = {blocks: halves(west, 0), blocks + 1: halves(east, 0)}
    for t in range(blocks):
        at = slice(t * LANES, (t + 1) * LANES)
        y = spread_out(rim_tables, nb_ref, coef_ref, at, [y_ref[v, :, at] for v in range(2)])
        for v in range(2):
            s = state_ref[v, :, at]
            t_own[v, :, at] = 0.5 * s + y[v] * (1.0 / 6.0)
            part_ref[v, :, at] = 0.5 * s + y[v] * (1.0 / 3.0)
    tables = blocks_of(t_own, blocks)
    tables.update(t_tables)
    for t in range(blocks):
        at = slice(t * LANES, (t + 1) * LANES)
        total = coef_total(nb_ref, coef_ref, at)
        z = spread_out(tables, nb_ref, coef_ref, at, [-total * r for r in tables[t]])
        edges = []
        for v in range(2):
            s = state_ref[v, :, at]
            h = part_ref[v, :, at] + (vert_ref[v] * (1.0 / 6.0)) * vertical(s)
            part_ref[v, :, at] = (s + z[v]) + vert_ref[v] * vertical(h)
            edges.append((h[0:1], s[0:1], h[7:8], s[7:8]))
        edge_ref[:, at] = jnp.concatenate([edges[v][i] for i in range(4) for v in range(2)], axis=0)
    lev = lax.axis_index("lev")
    width = to1.shape[1]
    pieces = cells // width
    everything = [edge_ref[:, i * width : (i + 1) * width] for i in range(pieces)]
    for shift, ref in enumerate((to1, to2, to3), start=1):
        at = pl.ds(pl.multiple_of((lev + shift) % pieces * width, width), width)
        rows = [part_ref[0, :, at], part_ref[1, :, at]]
        rows += [edge_ref[:, at]] if shift == 2 else everything
        ref[...] = jnp.concatenate(rows, axis=0).astype(jnp.bfloat16)


def finish_kernel(
    vert_ref, part_ref, edge_ref, from1, from2, from3, day_ref, cos_ref, owner_ref, wlw_ref, wsw_ref, gw_ref,
    new_ref, heat_ref, flux_ref, whole, edges, feat, acc, gwb, tot,
):
    lev = lax.axis_index("lev")
    count = edges.shape[0]
    width = from1.shape[1]
    cells = part_ref.shape[2]
    mine = pl.ds(pl.multiple_of(lev * width, width), width)
    for v in range(2):
        whole[v, pl.ds(pl.multiple_of(lev * 8, 8), 8), :] = part_ref[v, :, mine]
    edges[lev] = edge_ref[:, mine]
    for shift, ref in enumerate((from1, from2, from3), start=1):
        source = (lev + count - shift) % count
        got = ref[...].astype(jnp.float32)
        for v in range(2):
            whole[v, pl.ds(pl.multiple_of(source * 8, 8), 8), :] = got[8 * v : 8 * v + 8]
        if shift == 2:
            edges[source] = got[16:24]
        else:
            for i in range(count):

                @pl.when(lev == i)
                def _():
                    edges[source] = got[16 + 8 * i : 24 + 8 * i]

    for v in range(2):
        c = vert_ref[v]
        a = c * (1.0 / 6.0)
        for b in range(1, count):
            h_low, s_low = edges[b - 1, 4 + v : 5 + v, :], edges[b - 1, 6 + v : 7 + v, :]
            h_high, s_high = edges[b, v : v + 1, :], edges[b, 2 + v : 3 + v, :]
            r = 8 * b
            whole[v, r : r + 1, :] += c * (h_low - 2.0 * a * s_low + a * s_high)
            whole[v, r + 1 : r + 2, :] += (c * a) * s_low
            whole[v, r - 1 : r, :] += c * (h_high - 2.0 * a * s_high + a * s_low)
            whole[v, r - 2 : r - 1, :] += (c * a) * s_high
        feat[v * 8 * count : (v + 1) * 8 * count] = whole[v].astype(jnp.bfloat16)

    below = from1[16:, :].astype(jnp.float32)
    above = from3[16:, :].astype(jnp.float32)
    below = jnp.where(lev > 0, below, 0.0)
    above = jnp.where(lev < count - 1, above, 0.0)
    below = jnp.concatenate([below[8 * i : 8 * i + 8] for i in range(count)], axis=1)
    above = jnp.concatenate([above[8 * i : 8 * i + 8] for i in range(count)], axis=1)
    has_below = jnp.where(lev > 0, 1.0, 0.0)
    has_above = jnp.where(lev < count - 1, 1.0, 0.0)
    for v in range(2):
        c = vert_ref[v]
        a = c * (1.0 / 6.0)
        h_low, s_low = below[4 + v : 5 + v], below[6 + v : 7 + v]
        h_high, s_high = above[v : v + 1], above[2 + v : 3 + v]
        s_first, s_last = edge_ref[2 + v : 3 + v, :], edge_ref[6 + v : 7 + v, :]
        new_ref[v] = part_ref[v]
        new_ref[v, 0:1, :] += c * (h_low - 2.0 * a * s_low + (has_below * a) * s_first)
        new_ref[v, 1:2, :] += (c * a) * s_low
        new_ref[v, 7:8, :] += c * (h_high - 2.0 * a * s_high + (has_above * a) * s_last)
        new_ref[v, 6:7, :] += (c * a) * s_high

    sun = (day_ref[...].astype(jnp.float32) * cos_ref[...]).astype(jnp.bfloat16).astype(jnp.float32)
    radiate_body(
        8 * count, feat, sun, owner_ref, wlw_ref, wsw_ref, gw_ref, heat_ref, flux_ref, acc, gwb, tot
    )


def radiate_body(
    levels, feat_ref, sun, owner_ref, wlw_ref, wsw_ref, gw_ref, heat_ref, flux_ref, acc, gwb, tot
):
    cols = feat_ref.shape[1]
    spectral = gw_ref.shape[1]
    owners, cap = flux_ref.shape
    groups = spectral // 8
    chunk = 16
    scale = -1.5 / levels * LOG2E
    for b in range(2):
        wide = jnp.broadcast_to(gw_ref[b : b + 1, :], (spectral, spectral))
        gwb[b] = jnp.transpose(wide)
        tot[b, 0] = jnp.broadcast_to(
            jnp.sum(gwb[b].reshape(groups, 8, spectral), axis=0)[:, :1], (8, cols)
        )
        acc[b] = jnp.zeros((spectral, cols), jnp.float32)

    def level(l, carry):
        for b, w_ref in enumerate((wlw_ref, wsw_ref)):
            w = w_ref[:, pl.ds(pl.multiple_of(l * spectral, spectral), spectral)]
            x = lax.dot_general(
                w, feat_ref[...], (((0,), (0,)), ((), ())), preferred_element_type=jnp.float32
            )
            part = jnp.zeros((8, cols), jnp.float32)
            for r in range(0, spectral, chunk):
                xs = x[r : r + chunk]
                e = jnp.exp2(jnp.abs(xs) * -LOG2E)
                total = acc[b, r : r + chunk] + (jnp.maximum(xs, 0.0) + jnp.log(1.0 + e))
                acc[b, r : r + chunk] = total
                passed = jnp.exp2(total * scale)
                weight = jnp.concatenate([gwb[b, r : r + chunk]] * (cols // spectral), axis=1)
                passed = passed * weight
                for i in range(0, chunk, 8):
                    part = part + passed[i : i + 8]
            tot[b, l + 1] = part
        return carry

    lax.fori_loop(0, levels, level, 0)
    fraction = levels / spectral
    heats = []
    for b in range(2):
        heats.append(fraction * jnp.sum(tot[b, :levels] - tot[b, 1:], axis=1))
    heat_ref[...] = (sun * heats[1] - heats[0]).astype(jnp.bfloat16)
    bottoms = [jnp.sum(tot[b, levels], axis=0, keepdims=True) / spectral for b in range(2)]
    surface = bottoms[0] + sun * bottoms[1]
    scatter(surface, owner_ref[...], flux_ref, owners, cap, cols)


def scatter(surface, slot, flux_ref, owners, cap, cols):
    high = surface.astype(jnp.bfloat16).astype(jnp.float32)
    rest = surface - high
    mid = rest.astype(jnp.bfloat16).astype(jnp.float32)
    low = rest - mid
    owner = slot // cap
    within = slot - owner * cap
    mine = lax.broadcasted_iota(jnp.int32, (owners, cols), 0) == owner
    terms = jnp.concatenate([jnp.where(mine, term, 0.0) for term in (high, mid, low)], axis=0)
    place = lax.broadcasted_iota(jnp.int32, (cap, cols), 0) == within
    place = jnp.where(place, 1.0, 0.0).astype(jnp.bfloat16)
    out = lax.dot_general(
        terms.astype(jnp.bfloat16),
        place,
        (((1,), (1,)), ((), ())),
        preferred_element_type=jnp.float32,
    )
    flux_ref[...] = (out[:owners] + out[owners : 2 * owners]) + out[2 * owners :]


def call(kernel, outs, scratch, *args, name, scalars=0, cost=None):
    vmem = pl.BlockSpec(memory_space=pltpu.VMEM)
    smem = pl.BlockSpec(memory_space=pltpu.SMEM)
    return pl.pallas_call(
        kernel,
        in_specs=[smem] * scalars + [vmem] * (len(args) - scalars),
        out_specs=[vmem] * len(outs),
        out_shape=[jax.ShapeDtypeStruct(*out) for out in outs],
        scratch_shapes=[pltpu.VMEM(*s) for s in scratch],
        cost_estimate=cost,
        name=name,
    )(*args)


def swap(count, distance, flip):
    pairs = []
    for i in range(count):
        up = (i % (2 * distance) < distance) != flip
        pairs.append((i, (i + distance if up else i - distance) % count))
    return pairs


def on_device(
    state,
    neighbours,
    edge_coef,
    send_lists,
    vert_coef,
    w_lw,
    w_sw,
    g_weight,
    day,
    cos_zenith,
    owner_map,
):
    f32, bf16 = jnp.float32, jnp.bfloat16
    dom, lev = lax.axis_size("dom"), lax.axis_size("lev")
    cells = state.shape[2]
    levels = state.shape[1] * lev
    cols = cells // lev
    spectral = g_weight.shape[1]
    near_a, near_b, far_a, far_b, own = call(
        send_kernel,
        [((48, LANES), f32)] * 2 + [((16, LANES), f32)] * 2 + [((2, 2, 8, LANES), f32)],
        [((8, cells), jnp.int32), ((8, cells), f32)],
        state, neighbours, edge_coef, send_lists,
        name="send",
    )
    near_a = lax.ppermute(near_a, "dom", swap(dom, 1, False))
    near_b = lax.ppermute(near_b, "dom", swap(dom, 1, True))
    far_a = lax.ppermute(far_a, "dom", swap(dom, 2, False))
    far_b = lax.ppermute(far_b, "dom", swap(dom, 2, True))
    (inner,) = call(
        inner_kernel, [(state.shape, f32)], [], state, neighbours, edge_coef,
        name="inner",
        cost=pl.CostEstimate(flops=2000000, bytes_accessed=200000, transcendentals=0),
    )
    part, edge, to1, to2, to3 = call(
        step_kernel,
        [(state.shape, f32), ((8, cells), f32), ((16 + 8 * lev, cols), bf16), ((24, cols), bf16), ((16 + 8 * lev, cols), bf16)],
        [(state.shape, f32)],
        vert_coef, state, neighbours, edge_coef, inner, own, near_a, near_b, far_a, far_b,
        name="step", scalars=1,
    )
    turn = lambda x, shift: lax.ppermute(x, "lev", [(i, (i + shift) % lev) for i in range(lev)])
    new_state, heating, flux = call(
        finish_kernel,
        [(state.shape, f32), ((levels, cols), bf16), ((dom, 2 * cols // dom), f32)],
        [
            ((2, levels, cols), f32), ((lev, 8, cols), f32), ((2 * levels, cols), bf16),
            ((2, spectral, cols), f32), ((2, spectral, spectral), f32), ((2, levels + 1, 8, cols), f32),
        ],
        vert_coef, part, edge, turn(to1, 1), turn(to2, 2), turn(to3, 3),
        day.reshape(1, cols), cos_zenith.reshape(1, cols), owner_map.reshape(1, cols),
        w_lw, w_sw, g_weight,
        name="finish", scalars=1,
    )
    owner_flux = lax.all_to_all(flux, "dom", split_axis=0, concat_axis=0, tiled=True)
    return (new_state, heating, owner_flux.reshape(-1))


def solution(mesh):
    placed = (
        P(None, "lev", "dom"),
        P(None, "dom"),
        P(None, "dom"),
        P("dom", None, None),
        P(),
        P(),
        P(),
        P(),
        P(("dom", "lev")),
        P(("dom", "lev")),
        P(("dom", "lev")),
    )
    return jax.shard_map(
        on_device,
        mesh=mesh,
        in_specs=placed,
        out_specs=(P(None, "lev", "dom"), P(None, ("dom", "lev")), P(("dom", "lev"))),
        check_vma=False,
    )
```

time: 150 us -> 50.8 us (0.34)
  local copies, waits for them, and re-layouts: 90.7 us -> 2.38 us
  starting transfers between devices: 23.6 us -> 10.6 us
  Pallas kernels: 12.3 us -> 20.9 us
  other arithmetic: 8.07 us -> 0.66 us
    gather x34 -> x0, local copies, waits for them, and re-layouts: 80.3 us -> none  [the longest x28 77.2 us: tendency(): picked = jnp.take(extended, safe_links[neighbour], axis=2)]
    ppermute x8 -> x7, starting transfers between devices: 20.3 us -> 10.6 us  [the longest x1 3.54 us: on_device(): near_b = lax.ppermute(near_b, 'dom', swap(dom, 1, True))]
    pallas_call x1 -> x4, Pallas kernels: 12.3 us -> 20.9 us  [call(): pl.pallas_call(kernel, in_specs=[smem] * scalars + [vmem] * (len(args) -...]
    concatenate x2 -> x0, other arithmetic: 4.65 us -> none  [tendency(): jnp.concatenate([fields, bordered[:, :, :halo_cells], bordered[:, :, 3 *...]
    ppermute x8 -> x7, waiting for transfers between devices: 0.02 us -> 4.5 us  [the longest x3 2.42 us: on_device(): lax.ppermute(x, 'lev', [(i, (i + shift) % lev) for i in range(lev)])]
    all_to_all x1 -> x0, waiting for transfers between devices: 3.32 us -> none  [on_device(): lax.all_to_all(new_state.astype(jnp.bfloat16), 'lev', split_axis=2, conca...]
    all_to_all x1 -> x0, starting transfers between devices: 3.26 us -> none  [on_device(): lax.all_to_all(new_state.astype(jnp.bfloat16), 'lev', split_axis=2, conca...]
    unnamed x83 -> x14, local copies, waits for them, and re-layouts: 4.03 us -> 1.22 us
  transfers between devices with their start and end apart: 9 -> 7, of which waited for: 1 -> 3; matrix products, arithmetic and copies ran while one was open for 58% -> 0% of each run, Pallas kernels for 0% -> 5%
where the time goes in v2:
time: 50.8 us; the launch traced here: 50.5 us
  Pallas kernels  20.9 us (41%)
  blocking collectives  10.7 us (21%)
  starting transfers between devices  10.6 us (21%)
  waiting for transfers between devices  4.5 us (9%)
  local copies, waits for them, and re-layouts  2.38 us (5%)
  between operations  0.69 us (1%)
  other arithmetic  0.66 us (1%)
    pallas_call x4, Pallas kernels, call(): pl.pallas_call(kernel, in_specs=[smem] * scalars + [vmem] * (len(args) -...  20.9 us
    all_to_all x1, blocking collectives, on_device(): lax.all_to_all(flux, 'dom', split_axis=0, concat_axis=0, tiled=True)  10.7 us
    ppermute x1, starting transfers between devices, on_device(): near_b = lax.ppermute(near_b, 'dom', swap(dom, 1, True))  3.54 us
    ppermute x3, starting transfers between devices, on_device(): lax.ppermute(x, 'lev', [(i, (i + shift) % lev) for i in range(lev)])  3.23 us
    ppermute x1, starting transfers between devices, on_device(): near_a = lax.ppermute(near_a, 'dom', swap(dom, 1, False))  2.97 us
    ppermute x3, waiting for transfers between devices, on_device(): lax.ppermute(x, 'lev', [(i, (i + shift) % lev) for i in range(lev)])  2.42 us
    ppermute x1, waiting for transfers between devices, on_device(): far_b = lax.ppermute(far_b, 'dom', swap(dom, 2, True))  1.8 us
    unnamed x14, local copies, waits for them, and re-layouts  1.22 us
  transfers between devices with their start and end apart: 7, of which 3 were waited for; matrix products, arithmetic and copies ran while one was open for 0% of the time, Pallas kernels for 5%

profile of v2, /device:TPU:0, one launch (start us, length us, event | category | flops | bytes accessed | tf_op | source)
XLA Modules:
  0.0 50.5 jit_solution(14731025886487910237)
XLA Ops:
  0.6 2.0 %send.1 = (f32[48,128]{1,0:T(8,128)}, f32[48,128]{1,0:T(8,128)}, f32[16,128]{1,0:T(8,128)}, f32[16,128]{1,0:T(8,128)}, f32[2,2,8,128]{3,2,1,0:T(8,128)}) custom-call(f32[2,8,1024]{2,1,0:T(8,128)} %state_ref.5, s32[7,1024]{1,0:T(8,128)} %nb_ref.5, f32[7,1024]{1,0:T(8,128)} %coef_ref.5, s32[1,2,128]{2,1,0:T(2,128)} %lists_ref.1), custom_call_target="tpu_custom_call" | custom-call | tf_op jit(solution)/shard_map/send/pallas_call | solution.py:309
  2.7 3.0 %collective-permute-start = (f32[48,128]{1,0:T(8,128)}, f32[48,128]{1,0:T(8,128)S(1)}, u32[]{:S(2)}, u32[]{:S(2)}) collective-permute-start(f32[48,128]{1,0:T(8,128)} %get-tuple-element.17), channel_id=1, source_target_pairs={{0,4},{4,0},{8,12},{12,8},{16,20},{20,16},{24,28},{28,24},{1,5},{5... | collective-permute-start | bytes 73736 | tf_op jit(solution)/shard_map/ppermute | solution.py:354
  5.6 3.5 %collective-permute-start.1 = (f32[48,128]{1,0:T(8,128)}, f32[48,128]{1,0:T(8,128)S(1)}, u32[]{:S(2)}, u32[]{:S(2)}) collective-permute-start(f32[48,128]{1,0:T(8,128)} %get-tuple-element.18), channel_id=1, source_target_pairs={{0,28},{4,8},{8,4},{12,16},{16,12},{20,24},{24,20},{28,0},{1,29},{... | collective-permute-start | bytes 73736 | tf_op jit(solution)/shard_map/ppermute | solution.py:355
  9.2 0.9 %collective-permute-start.3 = (f32[16,128]{1,0:T(8,128)}, f32[16,128]{1,0:T(8,128)S(1)}, u32[]{:S(2)}, u32[]{:S(2)}) collective-permute-start(f32[16,128]{1,0:T(8,128)} %get-tuple-element.20), channel_id=1, source_target_pairs={{0,24},{4,28},{8,16},{12,20},{16,8},{20,12},{24,0},{28,4},{1,25},{... | collective-permute-start | bytes 24584 | tf_op jit(solution)/shard_map/ppermute | solution.py:357
  10.1 2.7 %inner.1.y_ref = f32[2,8,1024]{2,1,0:T(8,128)} custom-call(f32[2,8,1024]{2,1,0:T(8,128)} %state_ref.5, s32[7,1024]{1,0:T(8,128)} %nb_ref.5, f32[7,1024]{1,0:T(8,128)} %coef_ref.5), custom_call_target="tpu_custom_call" | custom-call | flops 2000000 | bytes 200000 | tf_op jit(solution)/shard_map/inner/pallas_call | solution.py:309
  12.8 0.3 collective-permute-done.2.far_a
  13.0 1.8 %collective-permute-done.3.far_b = f32[16,128]{1,0:T(8,128)S(1)} collective-permute-done((f32[16,128]{1,0:T(8,128)}, f32[16,128]{1,0:T(8,128)S(1)}, u32[]{:S(2)}, u32[]{:S(2)}) %collective-permute-start.3) | collective-permute-done | bytes 8224 | tf_op jit(solution)/shard_map/ppermute | solution.py:357
  14.9 0.0 collective-permute-done.near_a
  14.9 0.0 collective-permute-done.1.near_b
  14.9 0.6 %copy-done.6 = f32[16,128]{1,0:T(8,128)} copy-done((f32[16,128]{1,0:T(8,128)}, f32[16,128]{1,0:T(8,128)S(1)}, u32[]{:S(2)}) %copy-start.6) | copy-done | bytes 8216
  15.4 0.0 copy-done
  15.5 0.0 copy-done.1
  15.5 3.6 %step.1 = (f32[2,8,1024]{2,1,0:T(8,128)}, f32[8,1024]{1,0:T(8,128)}, bf16[48,256]{1,0:T(8,128)(2,1)}, bf16[24,256]{1,0:T(8,128)(2,1)}, bf16[48,256]{1,0:T(8,128)(2,1)}) custom-call(f32[2]{0:T(128)} %vert_ref.3, f32[2,8,1024]{2,1,0:T(8,128)} %state_ref.5, s32[7,1024]{1,0:T(8,128)} %nb_ref.5, f32[7,1024]{1,0:T(8,128)} %coef_ref.5, f32[2,8,1024]{2,1,0:T(8,128)} %inner.1.y_ref, ...), custom_call_target="tpu_custom_call" | custom-call | tf_op jit(solution)/shard_map/step/pallas_call | solution.py:309
  19.1 1.7 %collective-permute-start.6 = (bf16[48,256]{1,0:T(8,128)(2,1)}, bf16[48,256]{1,0:T(8,128)(2,1)S(1)}, u32[]{:S(2)}, u32[]{:S(2)}) collective-permute-start(bf16[48,256]{1,0:T(8,128)(2,1)} %get-tuple-element.25), channel_id=1, source_target_pairs={{0,3},{1,0},{2,1},{3,2},{4,7},{5,4},{6,5},{7,6},{8,11},{9,8},{10,9... | collective-permute-start | bytes 73736 | tf_op jit(solution)/shard_map/ppermute | solution.py:370
  20.9 1.5 %collective-permute-start.5 = (bf16[24,256]{1,0:T(8,128)(2,1)}, bf16[24,256]{1,0:T(8,128)(2,1)S(1)}, u32[]{:S(2)}, u32[]{:S(2)}) collective-permute-start(bf16[24,256]{1,0:T(8,128)(2,1)} %get-tuple-element.24), channel_id=1, source_target_pairs={{0,2},{1,3},{2,0},{3,1},{4,6},{5,7},{6,4},{7,5},{8,10},{9,11},{10,... | collective-permute-start | bytes 36872 | tf_op jit(solution)/shard_map/ppermute | solution.py:370
  22.4 2.4 %collective-permute-done.5.from2 = bf16[24,256]{1,0:T(8,128)(2,1)S(1)} collective-permute-done((bf16[24,256]{1,0:T(8,128)(2,1)}, bf16[24,256]{1,0:T(8,128)(2,1)S(1)}, u32[]{:S(2)}, u32[]{:S(2)}) %collective-permute-start.5) | collective-permute-done | bytes 12320 | tf_op jit(solution)/shard_map/ppermute | solution.py:370
  24.8 0.6 %copy-done.4 = bf16[24,256]{1,0:T(8,128)(2,1)} copy-done((bf16[24,256]{1,0:T(8,128)(2,1)}, bf16[24,256]{1,0:T(8,128)(2,1)S(1)}, u32[]{:S(2)}) %copy-start.4) | copy-done | bytes 12312
  25.4 0.0 copy-done.2
  25.4 0.0 copy-done.3
  25.4 12.5 %finish.1 = (f32[2,8,1024]{2,1,0:T(8,128)}, bf16[32,256]{1,0:T(8,128)(2,1)}, f32[8,64]{1,0:T(8,128)}) custom-call(f32[2]{0:T(128)} %vert_ref.3, f32[2,8,1024]{2,1,0:T(8,128)} %get-tuple-element.21.part_ref, f32[8,1024]{1,0:T(8,128)} %get-tuple-element.22.edge_ref, bf16[48,256]{1,0:T(8,128)(2,1)} %copy-done.2, bf16[24,256]{1,0:T(8,128)(2,1)} %copy-done.4, ...), custom_call_target="tpu_custom_call" | custom-call | tf_op jit(solution)/shard_map/finish/pallas_call | solution.py:309
  37.9 10.7 %all_to_all.9 = f32[8,1,64]{2,1,0:T(1,128)S(1)} all-to-all(f32[8,1,64]{2,1,0:T(1,128)} %bitcast.6), channel_id=1, replica_groups=mesh['dom'=8,'lev'=4] {'dom'}, dimensions={0} | all-to-all | bytes 4096 | tf_op jit(solution)/shard_map/all_to_all | solution.py:383
  48.6 0.5 %broadcast.3 = f32[]{:T(128)} broadcast(f32[]{:T(128)} %constant.4), dimensions={} | broadcast | bytes 8 | tf_op jit(solution)/shard_map/all_to_all | solution.py:383
  49.1 0.7 %reduce.3 = f32[8,64]{1,0:T(8,128)S(1)} reduce(f32[8,1,64]{2,1,0:T(1,128)S(1)} %all_to_all.9, f32[]{:T(128)} %broadcast.3), dimensions={1}, to_apply=%all_to_all.7.reduce_sub_computation.3 | reduce | bytes 4100 | tf_op jit(solution)/shard_map/all_to_all | solution.py:383
  49.8 0.7 %reshape.24 = f32[512]{0:T(512)} reshape(f32[8,64]{1,0:T(8,128)S(1)} %reduce.3) | data formatting | bytes 4096 | tf_op jit(solution)/shard_map/reshape | solution.py:384
  (12 shorter events, 0.0 us)
Async XLA Ops:
  2.7 12.2 %collective-permute-start = (f32[48,128]{1,0:T(8,128)}, f32[48,128]{1,0:T(8,128)S(1)}, u32[]{:S(2)}, u32[]{:S(2)}) collective-permute-start(f32[48,128]{1,0:T(8,128)} %get-tuple-element.17), channel_id=1, source_target_pairs={{0,4},{4,0},{8,12},{12,8},{16,20},{20,16},{24,28},{28,24},{1,5},{5... | collective-permute-start | bytes 73736 | tf_op jit(solution)/shard_map/ppermute | solution.py:354
  5.6 9.2 %collective-permute-start.1 = (f32[48,128]{1,0:T(8,128)}, f32[48,128]{1,0:T(8,128)S(1)}, u32[]{:S(2)}, u32[]{:S(2)}) collective-permute-start(f32[48,128]{1,0:T(8,128)} %get-tuple-element.18), channel_id=1, source_target_pairs={{0,28},{4,8},{8,4},{12,16},{16,12},{20,24},{24,20},{28,0},{1,29},{... | collective-permute-start | bytes 73736 | tf_op jit(solution)/shard_map/ppermute | solution.py:355
  9.2 3.9 %collective-permute-start.2 = (f32[16,128]{1,0:T(8,128)}, f32[16,128]{1,0:T(8,128)S(1)}, u32[]{:S(2)}, u32[]{:S(2)}) collective-permute-start(f32[16,128]{1,0:T(8,128)} %get-tuple-element.19), channel_id=1, source_target_pairs={{0,8},{4,12},{8,0},{12,4},{16,24},{20,28},{24,16},{28,20},{1,9},{5... | collective-permute-start | bytes 24584 | tf_op jit(solution)/shard_map/ppermute | solution.py:356
  9.2 5.7 %collective-permute-start.3 = (f32[16,128]{1,0:T(8,128)}, f32[16,128]{1,0:T(8,128)S(1)}, u32[]{:S(2)}, u32[]{:S(2)}) collective-permute-start(f32[16,128]{1,0:T(8,128)} %get-tuple-element.20), channel_id=1, source_target_pairs={{0,24},{4,28},{8,16},{12,20},{16,8},{20,12},{24,0},{28,4},{1,25},{... | collective-permute-start | bytes 24584 | tf_op jit(solution)/shard_map/ppermute | solution.py:357
  13.0 1.8 %copy-start.5 = (f32[16,128]{1,0:T(8,128)}, f32[16,128]{1,0:T(8,128)S(1)}, u32[]{:S(2)}) copy-start(f32[16,128]{1,0:T(8,128)S(1)} %collective-permute-done.2.far_a) | copy-start | bytes 24580
  14.8 0.6 %copy-start.6 = (f32[16,128]{1,0:T(8,128)}, f32[16,128]{1,0:T(8,128)S(1)}, u32[]{:S(2)}) copy-start(f32[16,128]{1,0:T(8,128)S(1)} %collective-permute-done.3.far_b) | copy-start | bytes 24580
  14.9 0.6 %copy-start = (f32[48,128]{1,0:T(8,128)}, f32[48,128]{1,0:T(8,128)S(1)}, u32[]{:S(2)}) copy-start(f32[48,128]{1,0:T(8,128)S(1)} %collective-permute-done.near_a) | copy-start | bytes 73732
  14.9 0.6 %copy-start.1 = (f32[48,128]{1,0:T(8,128)}, f32[48,128]{1,0:T(8,128)S(1)}, u32[]{:S(2)}) copy-start(f32[48,128]{1,0:T(8,128)S(1)} %collective-permute-done.1.near_b) | copy-start | bytes 73732
  19.1 5.7 %collective-permute-start.4 = (bf16[48,256]{1,0:T(8,128)(2,1)}, bf16[48,256]{1,0:T(8,128)(2,1)S(1)}, u32[]{:S(2)}, u32[]{:S(2)}) collective-permute-start(bf16[48,256]{1,0:T(8,128)(2,1)} %get-tuple-element.23), channel_id=1, source_target_pairs={{0,1},{1,2},{2,3},{3,0},{4,5},{5,6},{6,7},{7,4},{8,9},{9,10},{10,1... | collective-permute-start | bytes 73736 | tf_op jit(solution)/shard_map/ppermute | solution.py:370
  19.1 5.7 %collective-permute-start.6 = (bf16[48,256]{1,0:T(8,128)(2,1)}, bf16[48,256]{1,0:T(8,128)(2,1)S(1)}, u32[]{:S(2)}, u32[]{:S(2)}) collective-permute-start(bf16[48,256]{1,0:T(8,128)(2,1)} %get-tuple-element.25), channel_id=1, source_target_pairs={{0,3},{1,0},{2,1},{3,2},{4,7},{5,4},{6,5},{7,6},{8,11},{9,8},{10,9... | collective-permute-start | bytes 73736 | tf_op jit(solution)/shard_map/ppermute | solution.py:370
  20.9 3.9 %collective-permute-start.5 = (bf16[24,256]{1,0:T(8,128)(2,1)}, bf16[24,256]{1,0:T(8,128)(2,1)S(1)}, u32[]{:S(2)}, u32[]{:S(2)}) collective-permute-start(bf16[24,256]{1,0:T(8,128)(2,1)} %get-tuple-element.24), channel_id=1, source_target_pairs={{0,2},{1,3},{2,0},{3,1},{4,6},{5,7},{6,4},{7,5},{8,10},{9,11},{10,... | collective-permute-start | bytes 36872 | tf_op jit(solution)/shard_map/ppermute | solution.py:370
  24.8 0.6 %copy-start.4 = (bf16[24,256]{1,0:T(8,128)(2,1)}, bf16[24,256]{1,0:T(8,128)(2,1)S(1)}, u32[]{:S(2)}) copy-start(bf16[24,256]{1,0:T(8,128)(2,1)S(1)} %collective-permute-done.5.from2) | copy-start | bytes 36868
  24.8 0.6 %copy-start.2 = (bf16[48,256]{1,0:T(8,128)(2,1)}, bf16[48,256]{1,0:T(8,128)(2,1)S(1)}, u32[]{:S(2)}) copy-start(bf16[48,256]{1,0:T(8,128)(2,1)S(1)} %collective-permute-done.4.from1) | copy-start | bytes 73732
  24.8 0.6 %copy-start.3 = (bf16[48,256]{1,0:T(8,128)(2,1)}, bf16[48,256]{1,0:T(8,128)(2,1)S(1)}, u32[]{:S(2)}) copy-start(bf16[48,256]{1,0:T(8,128)(2,1)S(1)} %collective-permute-done.6.from3) | copy-start | bytes 73732
